TPU v7x, 32 devices: a whole 2x2x4 slice. The times are simulated.
32 devices in a mesh: seq: 8 (over y, x, core), ctx: 4 (over z).
Axes of the slice: x: 2, y: 2, z: 4, core: 2. Of those that a mesh axis runs over, the one named last changes fastest.
Arguments:
- tokens: bfloat16 [4096, 4096], P(('seq', 'ctx')), may hold values from -30 to 30
- modality: int32 [4096], P(('seq', 'ctx')), may hold values from 0 to 1, as said below
- keep_mask: int32 [4096], P(('seq', 'ctx')), may hold values from 0 to 1, as said below
- positions: int32 [4096], P(('seq', 'ctx')), may hold values from 0 to 4095
- modal_table: float32 [2, 4096], replicated, may hold values from -3 to 3
- norm_gain: float32 [4096], replicated, may hold values from 0.1 to 1.9
- norm_bias: float32 [4096], replicated, may hold values from -3 to 3
- qkv_weight: bfloat16 [3, 4096, 4096], P(None, None, 'seq'), may hold values from -1 to 1
- out_weight: bfloat16 [4096, 4096], P('seq'), may hold values from -0.09375 to 0.09375
- mask_token: float32 [4096], replicated, may hold values from -4 to 4
Outputs:
- encoded: float32 [4096, 4096], P(('seq', 'ctx'))
Inputs may be any that keep to these rules, and one draw needn't show every extreme that they name: `modality`: 0 marks a video token and 1 a taxel token; ids come in aligned runs of 16 tokens; five eighths of the tokens are video, and all tokens of at least one device are taxel. `keep_mask`: exactly 256 video tokens and 768 taxel tokens are kept, 1024 in all; on at least one device every token is kept.
All inputs are finite; a program needn't handle non-finite values.
Results may differ from a plain program's by a relative error of at most 0.0075.
Values may be sent and summed in bfloat16 or wider, within the bound.
A program may use at most 64 MiB of HBM per device.

v0:
```python
import math

import jax
import jax.numpy as jnp
from jax import lax
from jax.sharding import PartitionSpec as P

HEAD_DIM = 128


EPSILON = 1e-06


def position_table(positions, feature_width):
    half_width = feature_width // 2
    frequency = jnp.exp(-math.log(10000.0) * jnp.arange(half_width, dtype=jnp.float32) / half_width)
    angles = positions.astype(jnp.float32)[:, None] * frequency[None, :]
    return jnp.concatenate([jnp.sin(angles), jnp.cos(angles)], axis=1)


def embed(tokens, modality, positions, modal_table):
    table_rows = jnp.where(modality[:, None] == 1, modal_table[1][None, :], modal_table[0][None, :])
    summed = tokens.astype(jnp.float32) + position_table(positions, tokens.shape[1]) + table_rows
    return summed.astype(jnp.bfloat16)


def layer_norm(embedded, norm_gain, norm_bias):
    values = embedded.astype(jnp.float32)
    row_mean = jnp.mean(values, axis=1, keepdims=True)
    centered = values - row_mean
    row_var = jnp.mean(centered * centered, axis=1, keepdims=True)
    return (centered * lax.rsqrt(row_var + EPSILON) * norm_gain + norm_bias).astype(jnp.bfloat16)


def local(
    tokens,
    modality,
    keep_mask,
    positions,
    modal_table,
    norm_gain,
    norm_bias,
    qkv_weight,
    out_weight,
    mask_token,
):
    tok_rows, feature_width = tokens.shape
    seq_count = lax.axis_size("seq")
    ctx_count = lax.axis_size("ctx")
    devices = seq_count * ctx_count
    slot_count = (tok_rows + devices - 1) // devices
    capacity = devices * slot_count
    own_rows = tok_rows // 4
    my_index = lax.axis_index("seq") * ctx_count + lax.axis_index("ctx")
    embedded = embed(tokens, modality, positions, modal_table)
    visible = keep_mask == 1
    own_count = jnp.sum(keep_mask)
    counts = lax.all_gather(own_count[None], ("seq", "ctx"), axis=0, tiled=True)
    starts = jnp.cumsum(counts) - counts
    my_start = starts[my_index]
    local_rank = jnp.cumsum(keep_mask) - 1
    global_rank = my_start + local_rank
    token_slot = jnp.where(
        visible, global_rank % devices * slot_count + local_rank // devices, capacity
    )
    slot_token = (
        jnp.zeros((capacity + 1,), jnp.int32)
        .at[token_slot]
        .set(jnp.arange(tok_rows, dtype=jnp.int32))[:capacity]
    )
    slot_used = jnp.zeros((capacity + 1,), jnp.bool_).at[token_slot].set(True)[:capacity]
    outgoing = jnp.where(slot_used[:, None], embedded[slot_token], jnp.zeros((), jnp.bfloat16))
    arriving = lax.all_to_all(outgoing, ("seq", "ctx"), split_axis=0, concat_axis=0, tiled=True)
    slot_index = jnp.arange(capacity, dtype=jnp.int32)
    source = slot_index // slot_count
    slot_place = slot_index % slot_count
    source_start = starts[source]
    source_count = counts[source]
    offset = (my_index - source_start) % devices + devices * slot_place
    usable = offset < source_count
    slot_row = jnp.where(usable, (source_start + offset) // devices, own_rows)
    row_slot = jnp.zeros((own_rows + 1,), jnp.int32).at[slot_row].set(slot_index)[:own_rows]
    balanced = arriving[row_slot]
    normed = layer_norm(balanced, norm_gain, norm_bias)
    triple = jnp.einsum(
        "rd,tdc->trc",
        lax.all_gather(normed, "seq", axis=0, tiled=True),
        qkv_weight,
        preferred_element_type=jnp.float32,
    ).astype(jnp.bfloat16)
    queries, key_rows, values = (triple[0], triple[1], triple[2])
    group_rows, local_width = queries.shape
    heads_here = local_width // HEAD_DIM
    score_scale = 1.0 / math.sqrt(HEAD_DIM)
    query_heads = queries.reshape(group_rows, heads_here, HEAD_DIM)
    run_max = jnp.full((heads_here, group_rows), -jnp.inf, jnp.float32)
    run_sum = jnp.zeros((heads_here, group_rows), jnp.float32)
    run_acc = jnp.zeros((heads_here, group_rows, HEAD_DIM), jnp.float32)
    key_piece = lax.all_gather(key_rows, "ctx", axis=0, tiled=True)
    value_piece = lax.all_gather(values, "ctx", axis=0, tiled=True)
    length = key_piece.shape[0]
    block_size = min(length, 1024)
    for first_key in range(0, length, block_size):
        last_key = min(first_key + block_size, length)
        key_block = key_piece[first_key:last_key].reshape(
            last_key - first_key, heads_here, HEAD_DIM
        )
        value_block = value_piece[first_key:last_key].reshape(
            last_key - first_key, heads_here, HEAD_DIM
        )
        scores = (
            jnp.einsum("ghd,khd->hgk", query_heads, key_block, preferred_element_type=jnp.float32)
            * score_scale
        )
        new_max = jnp.maximum(run_max, jnp.max(scores, axis=2))
        factor = jnp.exp(run_max - new_max)
        expanded = jnp.exp(scores - new_max[:, :, None])
        run_sum = run_sum * factor + jnp.sum(expanded, axis=2)
        run_acc = run_acc * factor[:, :, None] + jnp.einsum(
            "hgk,khd->hgd",
            expanded.astype(jnp.bfloat16),
            value_block,
            preferred_element_type=jnp.float32,
        )
        run_max = new_max
    run_max, run_sum, run_acc = (run_max, run_sum, run_acc)
    attended = (run_acc / run_sum[:, :, None]).astype(jnp.bfloat16)
    attended = jnp.transpose(attended, (1, 0, 2)).reshape(group_rows, local_width)
    projected = lax.psum_scatter(
        jnp.dot(attended, out_weight, preferred_element_type=jnp.float32).astype(jnp.bfloat16),
        "seq",
        scatter_dimension=0,
        tiled=True,
    ).astype(jnp.float32)
    finished = balanced.astype(jnp.float32) + projected
    returning = jnp.where(
        usable[:, None], finished[jnp.minimum(slot_row, own_rows - 1)], jnp.zeros((), jnp.float32)
    )
    returned = lax.all_to_all(
        returning.astype(jnp.bfloat16), ("seq", "ctx"), split_axis=0, concat_axis=0, tiled=True
    ).astype(returning.dtype)
    restored = returned[jnp.minimum(token_slot, capacity - 1)]
    return jnp.where(visible[:, None], restored, mask_token[None, :])


def solution(mesh):
    in_specs = (
        P(("seq", "ctx"), None),
        P(("seq", "ctx")),
        P(("seq", "ctx")),
        P(("seq", "ctx")),
        P(),
        P(),
        P(),
        P(None, None, "seq"),
        P("seq", None),
        P(),
    )
    out_specs = P(("seq", "ctx"), None)
    return jax.shard_map(local, mesh=mesh, in_specs=in_specs, out_specs=out_specs, check_vma=False)
```

profile of v0, /device:TPU:0, one launch (start us, length us, event | category | flops | bytes accessed | tf_op | source)
XLA Modules:
  0.0 286.1 jit_solution(238786534744346636)
XLA Ops:
  6.6 1.4 reduce_sum.38
  7.9 0.8 dynamic-update-slice
  8.7 42.0 %all-reduce = s32[32]{0:T(128)S(1)} all-reduce(s32[32]{0:T(128)S(1)} %dynamic-update-slice), channel_id=1, replica_groups=mesh['seq'=8,'ctx'=4] {'seq','ctx'}, use_global_device_ids=true, to_apply=%add | all-reduce | flops 32 | bytes 256
  50.7 0.1 copy.19
  50.7 0.1 reduce-window.18
  50.8 0.1 reduce
  50.9 0.8 copy.20
  51.7 0.2 reduce-window.19
  51.9 0.1 add_reduce_fusion
  52.0 0.6 dynamic_slice.3
  52.6 1.3 compare_select_fusion.3
  53.9 1.0 scatter_custom_fusion.1
  54.9 0.7 convert_element_type.46
  55.6 0.9 fusion.74
  56.4 0.7 broadcast_compare_fusion
  57.1 3.7 %multiply_sine_fusion = (f32[128,2048]{1,0:T(8,128)S(1)}, f32[128,2048]{1,0:T(8,128)S(1)}) fusion(f32[2048]{0:T(1024)S(1)} %multiply_exponential_fusion, f32[128]{0:T(128)S(1)} %convert_element_type.46), kind=kLoop, calls=%fused_computation.24 | loop fusion | flops 262144 | bytes 2105856 | tf_op jit(solution)/shard_map/sin | solution.py:18
  60.8 0.4 fusion.5
  61.2 1.2 gather_fusion.2
  62.4 0.4 gather.32
  62.8 1.0 scatter_custom_fusion
  63.9 0.1 broadcast_in_dim.135
  64.0 1.5 broadcast_select_fusion.1
  65.5 4.4 %all-to-all-start = ((bf16[32,4,4096]{2,1,0:T(4,128)(2,1)}), bf16[32,4,4096]{2,1,0:T(4,128)(2,1)S(1)}, u32[]{:S(2)}, u32[]{:S(2)}) async-start(bf16[32,4,4096]{2,1,0:T(4,128)(2,1)} %broadcast_select_fusion.1), calls=%async_computation | async-start | bytes 2097152 | tf_op jit(solution)/shard_map/all_to_all | solution.py:73
  69.9 0.1 fusion.49
  70.1 1.2 gather_fusion
  71.3 1.2 gather_fusion.1
  72.5 0.1 copy.21
  72.7 0.1 copy.22
  72.8 0.2 fusion.51
  73.0 1.0 scatter_custom_fusion.2
  74.0 20.8 %all-to-all-done = bf16[32,4,4096]{2,1,0:T(4,128)(2,1)S(1)} async-done(((bf16[32,4,4096]{2,1,0:T(4,128)(2,1)}), bf16[32,4,4096]{2,1,0:T(4,128)(2,1)S(1)}, u32[]{:S(2)}, u32[]{:S(2)}) %all-to-all-start) | async-done | bytes 1048608 | tf_op jit(solution)/shard_map/all_to_all | solution.py:73
  94.8 0.3 all_to_all.11
  95.1 0.7 gather_fusion.3
  95.8 0.2 convert_reduce_fusion
  96.0 0.3 fusion.32
  96.2 0.9 fusion.35
  97.1 0.2 all-gather.8.cloned.1.call-start
  97.4 27.7 %all-gather.6.cloned.1.call-done = bf16[256,4096]{1,0:T(8,128)(2,1)} async-done(((bf16[32,4096]{1,0:T(8,128)(2,1)}), bf16[256,4096]{1,0:T(8,128)(2,1)}) %all-gather.6.cloned.1.call-update) | async-done | bytes 2097168 | tf_op jit(solution)/shard_map/all_gather | solution.py:87
  125.0 8.6 %fusion.13 = bf16[3,256,512]{2,1,0:T(8,128)(2,1)S(1)} fusion(bf16[3,4096,512]{2,1,0:T(8,128)(2,1)} %param.17, bf16[256,4096]{1,0:T(8,128)(2,1)} %all-gather.6.cloned.1.call-done), kind=kOutput, calls=%fused_computation.26 | convolution fusion | flops 3221618688 | bytes 15466496 | tf_op jit(solution)/shard_map/rd,tdc->trc/dot_general | solution.py:85
  133.6 0.9 fusion.73
  134.6 0.7 all-gather.10.cloned.1.call-update
  135.3 0.1 reshape_squeeze.3
  135.4 27.3 %all-gather.8.cloned.1.call-done = bf16[1,1024,512]{2,1,0:T(8,128)(2,1)} async-done(((bf16[1,256,512]{2,1,0:T(8,128)(2,1)}), bf16[1,1024,512]{2,1,0:T(8,128)(2,1)}) %all-gather.8.cloned.1.call-update) | async-done | bytes 1048592 | tf_op jit(solution)/shard_map/all_gather | solution.py:99
  162.7 1.3 reshape.321
  164.0 0.8 multiply_reduce_fusion
  164.8 0.9 fusion
  165.8 1.0 copy-done
  166.7 24.9 %all-gather.10.cloned.1.call-done = bf16[1,1024,512]{2,1,0:T(8,128)(2,1)} async-done(((bf16[1,256,512]{2,1,0:T(8,128)(2,1)}), bf16[1,1024,512]{2,1,0:T(8,128)(2,1)}) %all-gather.10.cloned.1.call-update) | async-done | bytes 1048592 | tf_op jit(solution)/shard_map/all_gather | solution.py:100
  191.6 1.5 copy.27
  193.1 3.4 %fusion.27 = bf16[256,4,128]{0,2,1:T(8,128)(2,1)S(1)} fusion(bf16[1024,4,128]{0,2,1:T(8,128)(2,1)S(1)} %bitcast.39, f32[4,256,1024]{2,1,0:T(8,128)} %copy-done, f32[4,256]{1,0:T(4,128)S(1)} %get-tuple-element.16, f32[256,4]{0,1:T(4,128)S(1)} %bitcast_add_fusion, f32[256,4]{0,1:T(4,128)S(1)} %multiply_bitcast_fusion), kind=kOutput, calls=%fused_computation.34 | convolution fusion | flops 271974400 | bytes 5517312 | tf_op jit(solution)/shard_map/hgk,khd->hgd/dot_general | solution.py:119
  196.5 0.1 copy-done.1
  196.6 2.6 convolution_convert_fusion
  199.2 0.1 gather.30
  199.3 0.1 sub.84
  199.5 40.4 %reduce-scatter.2.cloned.1.call-done = bf16[32,4096]{1,0:T(8,128)(2,1)} async-done(((bf16[256,4096]{1,0:T(8,128)(2,1)}), bf16[32,4096]{1,0:T(8,128)(2,1)}) %reduce-scatter.2.cloned.1.call-update) | async-done | bytes 262160 | tf_op jit(solution)/shard_map/reduce_scatter | solution.py:129
  239.9 1.0 convert_add_fusion
  240.9 1.2 gather_fusion.4
  242.1 0.4 gather.37
  242.5 1.6 select_convert_fusion
  244.2 4.6 %all-to-all-start.1 = ((bf16[32,4,4096]{2,1,0:T(4,128)(2,1)}), bf16[32,4,4096]{2,1,0:T(4,128)(2,1)S(1)}, u32[]{:S(2)}, u32[]{:S(2)}) async-start(bf16[32,4,4096]{2,1,0:T(4,128)(2,1)} %select_convert_fusion), calls=%async_computation.2 | async-start | bytes 2097152 | tf_op jit(solution)/shard_map/all_to_all | solution.py:139
  248.8 24.9 %all-to-all-done.1 = bf16[32,4,4096]{2,1,0:T(4,128)(2,1)S(1)} async-done(((bf16[32,4,4096]{2,1,0:T(4,128)(2,1)}), bf16[32,4,4096]{2,1,0:T(4,128)(2,1)S(1)}, u32[]{:S(2)}, u32[]{:S(2)}) %all-to-all-start.1) | async-done | bytes 1048608 | tf_op jit(solution)/shard_map/all_to_all | solution.py:139
  273.7 0.2 reshape.324
  273.9 2.5 gather_fusion.5
  276.4 3.2 %broadcast_select_fusion = f32[128,4096]{1,0:T(8,128)} fusion(f32[128,4096]{1,0:T(8,128)} %gather_fusion.5, f32[4096]{0:T(1024)S(1)} %copy-done.3, pred[128]{0:T(512)(128)(4,1)S(1)} %broadcast_compare_fusion.1), kind=kLoop, calls=%fused_computation.31 | loop fusion | flops 524288 | bytes 4210816 | tf_op jit(solution)/shard_map/jit(_where)/select_n | solution.py:143
  (39 shorter events, 0.3 us)
Async XLA Ops:
  6.5 54.3 %copy-start.2 = (bf16[128,4096]{1,0:T(8,128)(2,1)S(1)}, bf16[128,4096]{1,0:T(8,128)(2,1)}, u32[]{:S(2)}) copy-start(bf16[128,4096]{1,0:T(8,128)(2,1)} %param.10) | copy-start | bytes 3145732
  65.5 29.3 %all-to-all-start = ((bf16[32,4,4096]{2,1,0:T(4,128)(2,1)}), bf16[32,4,4096]{2,1,0:T(4,128)(2,1)S(1)}, u32[]{:S(2)}, u32[]{:S(2)}) async-start(bf16[32,4,4096]{2,1,0:T(4,128)(2,1)} %broadcast_select_fusion.1), calls=%async_computation | async-start | bytes 2097152 | tf_op jit(solution)/shard_map/all_to_all | solution.py:73
  69.9 55.1 %all-gather.6.cloned.1.call-start = ((), (), s32[]{:S(2)}) async-start(), calls=%async_computation.3 | async-start | bytes 2359296 | tf_op jit(solution)/shard_map/all_gather | solution.py:87
  74.0 22.3 %copy-start.4 = (f32[4096]{0:T(1024)S(1)}, f32[4096]{0:T(1024)}, u32[]{:S(2)}) copy-start(f32[4096]{0:T(1024)} %param.16) | copy-start | bytes 49156
  74.0 22.2 %copy-start.5 = (f32[4096]{0:T(1024)S(1)}, f32[4096]{0:T(1024)}, u32[]{:S(2)}) copy-start(f32[4096]{0:T(1024)} %param.15) | copy-start | bytes 49156
  97.1 65.5 %all-gather.8.cloned.1.call-start = ((), (), s32[]{:S(2)}) async-start(), calls=%async_computation.5 | async-start | bytes 1310720 | tf_op jit(solution)/shard_map/all_gather | solution.py:99
  134.5 57.1 %all-gather.10.cloned.1.call-start = ((), (), s32[]{:S(2)}) async-start(), calls=%async_computation.6 | async-start | bytes 1310720 | tf_op jit(solution)/shard_map/all_gather | solution.py:100
  135.3 104.6 %reduce-scatter.2.cloned.1.call-start = ((), (), s32[]{:S(2)}) async-start(), calls=%async_computation.4 | async-start | bytes 2359296 | tf_op jit(solution)/shard_map/reduce_scatter | solution.py:129
  164.8 1.9 copy-start
  193.1 3.5 %copy-start.1 = (bf16[512,4096]{1,0:T(8,128)(2,1)S(1)}, bf16[512,4096]{1,0:T(8,128)(2,1)}, u32[]{:S(2)}) copy-start(bf16[512,4096]{1,0:T(8,128)(2,1)} %param.18) | copy-start | bytes 12582916
  242.5 6.3 %copy-start.6 = (s32[128]{0:T(128)S(1)}, s32[128]{0:T(128)}, u32[]{:S(2)}) copy-start(s32[128]{0:T(128)} %param.12) | copy-start | bytes 1540
  244.2 29.5 %all-to-all-start.1 = ((bf16[32,4,4096]{2,1,0:T(4,128)(2,1)}), bf16[32,4,4096]{2,1,0:T(4,128)(2,1)S(1)}, u32[]{:S(2)}, u32[]{:S(2)}) async-start(bf16[32,4,4096]{2,1,0:T(4,128)(2,1)} %select_convert_fusion), calls=%async_computation.2 | async-start | bytes 2097152 | tf_op jit(solution)/shard_map/all_to_all | solution.py:139
  273.9 2.5 copy-start.3
Sparse Core Ops, SparseCore 0:
  97.3 27.7 all-gather.5
  134.6 27.9 all-gather.7
  164.2 27.3 all-gather.9
  199.3 40.4 reduce-scatter.1
where the time goes:
time: 288 us; the launch traced here: 286 us
  waiting for transfers between devices  167 us (58%)
  blocking collectives  42 us (15%)
  local copies, waits for them, and re-layouts  20.7 us (7%)
  other arithmetic  18.5 us (6%)
  matrix products  15.4 us (5%)
  between operations  13.5 us (5%)
  starting transfers between devices  9.34 us (3%)
    unnamed x1, blocking collectives  42 us
    reduce_scatter x1, waiting for transfers between devices, local(): lax.psum_scatter(jnp.dot(attended, out_weight, preferred_element_type=jnp...  40.4 us
    all_gather x1, waiting for transfers between devices, local(): lax.all_gather(normed, 'seq', axis=0, tiled=True)  27.7 us
    all_gather x1, waiting for transfers between devices, local(): key_piece = lax.all_gather(key_rows, 'ctx', axis=0, tiled=True)  27.3 us
    all_to_all x1, waiting for transfers between devices, local(): lax.all_to_all(returning.astype(jnp.bfloat16), ('seq', 'ctx'), split_axis...  24.9 us
    all_gather x1, waiting for transfers between devices, local(): value_piece = lax.all_gather(values, 'ctx', axis=0, tiled=True)  24.9 us
    all_to_all x1, waiting for transfers between devices, local(): lax.all_to_all(outgoing, ('seq', 'ctx'), split_axis=0, concat_axis=0, til...  20.8 us
    dot_general x1, matrix products, local(): jnp.einsum('rd,tdc->trc', lax.all_gather(normed, 'seq', axis=0, tiled=Tru...  8.61 us
  transfers between devices with their start and end apart: 6, of which 6 were waited for; matrix products, arithmetic and copies ran while one was open for 3% of the time, Pallas kernels for 0%

commit v1 on v0

v1 whole, which is shorter than its diff:
```python
import math

import jax
import jax.numpy as jnp
from jax import lax
from jax.experimental import pallas as pl
from jax.experimental.pallas import tpu as pltpu
from jax.sharding import PartitionSpec as P

HEAD_DIM = 128


EPSILON = 1e-06
MESH = pl.DeviceIdType.MESH


def position_table(positions, feature_width):
    half_width = feature_width // 2
    frequency = jnp.exp(-math.log(10000.0) * jnp.arange(half_width, dtype=jnp.float32) / half_width)
    angles = positions.astype(jnp.float32)[:, None] * frequency[None, :]
    return jnp.concatenate([jnp.sin(angles), jnp.cos(angles)], axis=1)


def embed(tokens, modality, positions, modal_table):
    table_rows = jnp.where(modality[:, None] == 1, modal_table[1][None, :], modal_table[0][None, :])
    summed = tokens.astype(jnp.float32) + position_table(positions, tokens.shape[1]) + table_rows
    return summed.astype(jnp.bfloat16)


def layer_norm(embedded, norm_gain, norm_bias):
    values = embedded.astype(jnp.float32)
    row_mean = jnp.mean(values, axis=1, keepdims=True)
    centered = values - row_mean
    row_var = jnp.mean(centered * centered, axis=1, keepdims=True)
    return (centered * lax.rsqrt(row_var + EPSILON) * norm_gain + norm_bias).astype(jnp.bfloat16)


def everyone():
    seq_count, ctx_count = lax.axis_size("seq"), lax.axis_size("ctx")

    def place():
        return lax.axis_index("seq") * ctx_count + lax.axis_index("ctx")

    return seq_count * ctx_count, place, lambda j: {"seq": j // ctx_count, "ctx": lax.rem(j, ctx_count)}


def along(axis):
    return lax.axis_size(axis), lambda: lax.axis_index(axis), lambda j: {axis: j}


def same_parity():
    return (
        lax.axis_size("seq") // 2,
        lambda: lax.axis_index("seq") // 2,
        lambda j: {"seq": 2 * j + lax.rem(lax.axis_index("seq"), 2)},
    )


def siblings():
    return (
        2,
        lambda: lax.rem(lax.axis_index("seq"), 2),
        lambda j: {"seq": lax.axis_index("seq") // 2 * 2 + j},
    )


def exchange(x, group, source, target, out_shape, collective_id):
    count, place, device_of = group

    def kernel(x_ref, out_ref, send_sem, recv_sem, own_sem):
        me = place()
        barrier = pltpu.get_barrier_semaphore()

        def greet(step, carry):
            peer = lax.rem(me + step, count)
            pl.semaphore_signal(barrier, inc=1, device_id=device_of(peer), device_id_type=MESH)
            return carry

        def push(step):
            peer = lax.rem(me + step, count)
            return pltpu.make_async_remote_copy(
                src_ref=source(x_ref, peer),
                dst_ref=target(out_ref, me),
                send_sem=send_sem.at[step],
                recv_sem=recv_sem.at[step],
                device_id=device_of(peer),
                device_id_type=MESH,
            )

        def start(step, carry):
            push(step).start()
            return carry

        def finish(step, carry):
            push(step).wait()
            return carry

        lax.fori_loop(1, count, greet, 0)
        own = pltpu.make_async_copy(source(x_ref, me), target(out_ref, me), own_sem)
        own.start()
        pl.semaphore_wait(barrier, count - 1)
        lax.fori_loop(1, count, start, 0)
        lax.fori_loop(1, count, finish, 0)
        own.wait()

    return pl.pallas_call(
        kernel,
        out_shape=jax.ShapeDtypeStruct(out_shape, x.dtype),
        in_specs=[pl.BlockSpec(memory_space=pltpu.VMEM)],
        out_specs=pl.BlockSpec(memory_space=pltpu.VMEM),
        scratch_shapes=[
            pltpu.SemaphoreType.DMA((count,)),
            pltpu.SemaphoreType.DMA((count,)),
            pltpu.SemaphoreType.DMA,
        ],
        compiler_params=pltpu.CompilerParams(collective_id=collective_id, has_side_effects=True),
    )(x)


def part(ref, j):
    return ref.at[j]


def whole(ref, j):
    return ref


def attend(triple):
    _, heads, rows, _ = triple.shape
    block = min(rows, 256)
    score_scale = 1.0 / math.sqrt(HEAD_DIM)

    def kernel(q_ref, k_ref, v_ref, out_ref):
        scores = (
            lax.dot_general(
                q_ref[...], k_ref[...], (((1,), (1,)), ((), ())), preferred_element_type=jnp.float32
            )
            * score_scale
        )
        expanded = jnp.exp(scores - jnp.max(scores, axis=1, keepdims=True))
        total = jnp.sum(expanded, axis=1, keepdims=True)
        summed = jnp.dot(expanded.astype(jnp.bfloat16), v_ref[...], preferred_element_type=jnp.float32)
        out_ref[...] = (summed / total).astype(jnp.bfloat16)

    return pl.pallas_call(
        kernel,
        grid=(heads, rows // block),
        out_shape=jax.ShapeDtypeStruct((heads, rows, HEAD_DIM), jnp.bfloat16),
        in_specs=[
            pl.BlockSpec((None, None, block, HEAD_DIM), lambda h, i: (0, h, i, 0)),
            pl.BlockSpec((None, None, rows, HEAD_DIM), lambda h, i: (1, h, 0, 0)),
            pl.BlockSpec((None, None, rows, HEAD_DIM), lambda h, i: (2, h, 0, 0)),
        ],
        out_specs=pl.BlockSpec((None, block, HEAD_DIM), lambda h, i: (h, i, 0)),
    )(triple, triple, triple)


def attend_by_head(triple):
    _, group_rows, local_width = triple.shape
    ctx = along("ctx")
    count = ctx[0]
    width = local_width // count
    heads = width // HEAD_DIM
    gathered = exchange(
        triple,
        ctx,
        lambda ref, j: ref.at[:, :, pl.ds(pl.multiple_of(j * width, HEAD_DIM), width)],
        lambda ref, j: ref.at[:, pl.ds(pl.multiple_of(j * group_rows, group_rows), group_rows), :],
        (3, count * group_rows, width),
        3,
    )
    if heads == 1:
        split = gathered[:, None]
    else:
        split = jnp.transpose(
            gathered.reshape(3, count * group_rows, heads, HEAD_DIM), (0, 2, 1, 3)
        )
    done = attend(split)
    if heads == 1:
        done = done[0]
    else:
        done = jnp.transpose(done, (1, 0, 2)).reshape(count * group_rows, width)
    return exchange(
        done,
        ctx,
        lambda ref, j: ref.at[pl.ds(pl.multiple_of(j * group_rows, group_rows), group_rows), :],
        lambda ref, j: ref.at[:, pl.ds(pl.multiple_of(j * width, HEAD_DIM), width)],
        (group_rows, local_width),
        4,
    )


def attend_by_row(triple):
    queries, key_rows, values = (triple[0], triple[1], triple[2])
    group_rows, local_width = queries.shape
    heads_here = local_width // HEAD_DIM
    score_scale = 1.0 / math.sqrt(HEAD_DIM)
    both = lax.all_gather(jnp.stack([key_rows, values]), "ctx", axis=1, tiled=True)
    length = both.shape[1]
    query_heads = queries.reshape(group_rows, heads_here, HEAD_DIM)
    key_heads = both[0].reshape(length, heads_here, HEAD_DIM)
    value_heads = both[1].reshape(length, heads_here, HEAD_DIM)
    scores = (
        jnp.einsum("ghd,khd->hgk", query_heads, key_heads, preferred_element_type=jnp.float32)
        * score_scale
    )
    expanded = jnp.exp(scores - jnp.max(scores, axis=2, keepdims=True))
    total = jnp.sum(expanded, axis=2, keepdims=True)
    summed = jnp.einsum(
        "hgk,khd->hgd",
        expanded.astype(jnp.bfloat16),
        value_heads,
        preferred_element_type=jnp.float32,
    )
    attended = (summed / total).astype(jnp.bfloat16)
    return jnp.transpose(attended, (1, 0, 2)).reshape(group_rows, local_width)


def local(
    tokens,
    modality,
    keep_mask,
    positions,
    modal_table,
    norm_gain,
    norm_bias,
    qkv_weight,
    out_weight,
    mask_token,
):
    tok_rows, feature_width = tokens.shape
    seq_count = lax.axis_size("seq")
    ctx_count = lax.axis_size("ctx")
    devices = seq_count * ctx_count
    slot_count = (tok_rows + devices - 1) // devices
    capacity = devices * slot_count
    own_rows = tok_rows // 4
    my_index = lax.axis_index("seq") * ctx_count + lax.axis_index("ctx")
    visible = keep_mask == 1
    own_count = jnp.sum(keep_mask)
    counts = exchange(
        jnp.full((1, 128), own_count, jnp.int32), everyone(), whole, part, (devices, 1, 128), 0
    )[:, 0, 0]
    index = jnp.arange(devices, dtype=jnp.int32)
    starts = jnp.sum(jnp.where(index[None, :] < index[:, None], counts[None, :], 0), axis=1)
    my_start = jnp.sum(jnp.where(index < my_index, counts, 0))
    token_index = jnp.arange(tok_rows, dtype=jnp.int32)
    local_rank = (
        jnp.sum(jnp.where(token_index[None, :] <= token_index[:, None], keep_mask[None, :], 0), axis=1) - 1
    )
    global_rank = my_start + local_rank
    token_slot = jnp.where(
        visible, global_rank % devices * slot_count + local_rank // devices, capacity
    )
    slot_index = jnp.arange(capacity, dtype=jnp.int32)
    slot_of_token = (token_slot[:, None] == slot_index[None, :]).astype(jnp.bfloat16)
    slot_place = slot_index % slot_count
    source_start = jnp.repeat(starts, slot_count)
    source_count = jnp.repeat(counts, slot_count)
    offset = (my_index - source_start) % devices + devices * slot_place
    usable = offset < source_count
    slot_row = jnp.where(usable, (source_start + offset) // devices, own_rows)
    row_of_slot = (
        slot_row[:, None] == jnp.arange(own_rows, dtype=jnp.int32)[None, :]
    ).astype(jnp.bfloat16)

    embedded = embed(tokens, modality, positions, modal_table)

    def pick(choice, rows, side):
        return lax.dot_general(
            choice, rows, (((side,), (0,)), ((), ())), preferred_element_type=jnp.float32
        )

    outgoing = pick(slot_of_token, embedded, 0).astype(jnp.bfloat16)
    slots = (devices, slot_count, feature_width)
    arriving = exchange(outgoing.reshape(slots), everyone(), part, part, slots, 1)
    balanced = pick(row_of_slot, arriving.reshape(capacity, feature_width), 0)
    normed = layer_norm(balanced, norm_gain, norm_bias)
    group = exchange(normed, along("seq"), whole, part, (seq_count,) + normed.shape, 2)
    group = group.reshape(seq_count * own_rows, feature_width)
    triple = jnp.einsum(
        "rd,tdc->trc", group, qkv_weight, preferred_element_type=jnp.float32
    ).astype(jnp.bfloat16)
    if triple.shape[2] % (ctx_count * HEAD_DIM) == 0:
        attended = attend_by_head(triple)
    else:
        attended = attend_by_row(triple)
    shares = jnp.dot(attended, out_weight, preferred_element_type=jnp.float32).astype(jnp.bfloat16)
    shares = shares.reshape(seq_count, own_rows, feature_width)
    shares = exchange(shares, along("seq"), part, part, shares.shape, 5)
    projected = jnp.sum(shares.astype(jnp.float32), axis=0).astype(jnp.bfloat16)
    returning = pick(row_of_slot, projected, 1).astype(jnp.bfloat16)
    returned = exchange(returning.reshape(slots), everyone(), part, part, slots, 6)
    restored = pick(slot_of_token, returned.reshape(capacity, feature_width), 1)
    return jnp.where(visible[:, None], embedded.astype(jnp.float32) + restored, mask_token[None, :])


def solution(mesh):
    in_specs = (
        P(("seq", "ctx"), None),
        P(("seq", "ctx")),
        P(("seq", "ctx")),
        P(("seq", "ctx")),
        P(),
        P(),
        P(),
        P(None, None, "seq"),
        P("seq", None),
        P(),
    )
    out_specs = P(("seq", "ctx"), None)
    return jax.shard_map(local, mesh=mesh, in_specs=in_specs, out_specs=out_specs, check_vma=False)
```

time: 288 us -> 205 us (0.71)
  Pallas kernels: 0 us -> 167 us
  waiting for transfers between devices: 167 us -> 0 us
  blocking collectives: 42 us -> 0 us
  between operations: 13.5 us -> 0.23 us
  local copies, waits for them, and re-layouts: 20.7 us -> 8.08 us
  starting transfers between devices: 9.34 us -> 0 us
  other arithmetic: 18.5 us -> 12.1 us
    pallas_call x0 -> x8, Pallas kernels: none -> 167 us  [the longest x7 162 us: exchange(): pl.pallas_call(kernel, out_shape=jax.ShapeDtypeStruct(out_shape, x.dtype)...]
    all_gather x3 -> x0, waiting for transfers between devices: 79.8 us -> none  [the longest x1 27.7 us: local(): lax.all_gather(normed, 'seq', axis=0, tiled=True)]
    all_to_all x2 -> x0, waiting for transfers between devices: 45.7 us -> none  [the longest x1 24.9 us: local(): lax.all_to_all(returning.astype(jnp.bfloat16), ('seq', 'ctx'), split_axis...]
    unnamed x1 -> x0, blocking collectives: 42 us -> none
    reduce_scatter x1 -> x0, waiting for transfers between devices: 40.4 us -> none  [local(): lax.psum_scatter(jnp.dot(attended, out_weight, preferred_element_type=jnp...]
    gather x11 -> x0, local copies, waits for them, and re-layouts: 9.25 us -> none  [the longest x1 2.53 us: local(): restored = returned[jnp.minimum(token_slot, capacity - 1)]]
    all_to_all x2 -> x0, starting transfers between devices: 9 us -> none  [the longest x1 4.6 us: local(): lax.all_to_all(returning.astype(jnp.bfloat16), ('seq', 'ctx'), split_axis...]
    select_n x8 -> x2, other arithmetic: 6.31 us -> 1.34 us  [the longest x1 1.32 us: local(): jnp.where(visible, global_rank % devices * slot_count + local_rank // dev...]
  transfers between devices with their start and end apart: 6 -> 0, of which waited for: 6 -> 0; matrix products, arithmetic and copies ran while one was open for 3% -> 0% of each run, Pallas kernels for 0% -> 0%
where the time goes in v1:
time: 205 us
  Pallas kernels  167 us (81%)
  matrix products  17.7 us (9%)
  other arithmetic  12.1 us (6%)
  local copies, waits for them, and re-layouts  8.08 us (4%)
    pallas_call x7, Pallas kernels, exchange(): pl.pallas_call(kernel, out_shape=jax.ShapeDtypeStruct(out_shape, x.dtype)...  162 us
    dot_general x1, matrix products, local(): jnp.einsum('rd,tdc->trc', group, qkv_weight, preferred_element_type=jnp.f...  9.5 us
    dot_general x1, matrix products, local(): jnp.dot(attended, out_weight, preferred_element_type=jnp.float32)  4.86 us
    pallas_call x1, Pallas kernels, attend(): pl.pallas_call(kernel, grid=(heads, rows // block), out_shape=jax.ShapeDt...  4.69 us

profile of v1, /device:TPU:0, one launch (start us, length us, event | category | flops | bytes accessed | tf_op | source)
XLA Modules:
  0.0 204.8 jit_solution(9327641025710852288)
XLA Ops:
  0.0 0.0 copy-start.1
  0.0 0.0 copy-start.6
  0.0 0.0 copy-start
  0.0 1.4 reduce_sum.66
  1.4 1.1 broadcast_in_dim.113.x_ref
  2.5 11.3 %shard_map.100 = s32[32,1,128]{2,1,0:T(1,128)} custom-call(s32[1,128]{1,0:T(1,128)} %broadcast_in_dim.113.x_ref), custom_call_target="tpu_custom_call" | custom-call | tf_op jit(solution)/shard_map/pallas_call | solution.py:106
  13.9 1.4 slice_reduce_fusion
  15.3 0.6 fusion.10
  15.9 0.8 select_reduce_fusion
  16.7 1.3 fusion.13
  18.0 0.7 convert_element_type.34
  18.7 3.7 %multiply_sine_fusion = (f32[128,2048]{1,0:T(8,128)S(1)}, f32[128,2048]{1,0:T(8,128)S(1)}) fusion(f32[2048]{0:T(1024)S(1)} %multiply_exponential_fusion, f32[128]{0:T(128)S(1)} %convert_element_type.34), kind=kLoop, calls=%fused_computation.9 | loop fusion | flops 262144 | bytes 2105856 | tf_op jit(solution)/shard_map/sin | solution.py:21
  22.4 0.0 copy-done.1
  22.4 0.0 copy-done.6
  22.4 0.0 copy-done
  22.4 0.4 fusion.2
  22.8 0.5 convolution_convert_fusion.2
  23.4 1.2 reshape.105.x_ref
  24.6 30.9 %shard_map.101 = bf16[32,4,4096]{2,1,0:T(4,128)(2,1)} custom-call(bf16[32,4,4096]{2,1,0:T(4,128)(2,1)} %reshape.105.x_ref), custom_call_target="tpu_custom_call" | custom-call | tf_op jit(solution)/shard_map/pallas_call | solution.py:106
  55.5 0.0 copy-start.3
  55.5 0.0 copy-start.4
  55.6 1.3 reshape.106
  56.9 0.1 select_reduce_fusion.1
  57.0 0.1 broadcast_in_dim.120
  57.1 0.1 reshape.103
  57.2 0.1 broadcast_in_dim.121
  57.3 0.1 reshape.104
  57.4 0.5 fusion.18
  57.9 0.2 multiply_reduce_fusion
  58.2 0.0 copy-done.3
  58.2 0.0 copy-done.4
  58.2 0.9 add_convert_fusion.x_ref
  59.1 26.6 %shard_map.102 = bf16[8,32,4096]{2,1,0:T(8,128)(2,1)} custom-call(bf16[32,4096]{1,0:T(8,128)(2,1)} %add_convert_fusion.x_ref), custom_call_target="tpu_custom_call" | custom-call | tf_op jit(solution)/shard_map/pallas_call | solution.py:106
  85.7 9.5 %fusion.3.x_ref = bf16[3,256,512]{2,1,0:T(8,128)(2,1)} fusion(bf16[256,4096,1]{1,0,2:T(8,128)(2,1)} %bitcast.21, bf16[3,4096,512]{2,1,0:T(8,128)(2,1)} %param.17), kind=kOutput, calls=%fused_computation.11 | convolution fusion | flops 3221618688 | bytes 15466496 | tf_op jit(solution)/shard_map/rd,tdc->trc/dot_general | solution.py:281
  95.2 20.2 %shard_map.103 = bf16[3,1024,128]{2,1,0:T(8,128)(2,1)} custom-call(bf16[3,256,512]{2,1,0:T(8,128)(2,1)} %fusion.3.x_ref), custom_call_target="tpu_custom_call" | custom-call | tf_op jit(solution)/shard_map/pallas_call | solution.py:106
  115.4 4.7 %shard_map.104 = bf16[1,1024,128]{2,1,0:T(8,128)(2,1)} custom-call(bf16[3,1,1024,128]{3,2,1,0:T(8,128)(2,1)} %bitcast.18, bf16[3,1,1024,128]{3,2,1,0:T(8,128)(2,1)} %bitcast.19, bf16[3,1,1024,128]{3,2,1,0:T(8,128)(2,1)} %bitcast.20), custom_call_target="tpu_custom_call" | custom-call | tf_op jit(solution)/shard_map/pallas_call | solution.py:145
  120.1 13.9 %shard_map.105 = bf16[256,512]{1,0:T(8,128)(2,1)} custom-call(bf16[1024,128]{1,0:T(8,128)(2,1)} %bitcast.23), custom_call_target="tpu_custom_call" | custom-call | tf_op jit(solution)/shard_map/pallas_call | solution.py:106
  133.9 4.9 %convolution_convert_fusion = bf16[256,4096]{1,0:T(8,128)(2,1)} fusion(bf16[256,512]{1,0:T(8,128)(2,1)} %shard_map.105, bf16[512,4096]{1,0:T(8,128)(2,1)} %param.18), kind=kOutput, calls=%fused_computation | convolution fusion | flops 1074790400 | bytes 6553600 | tf_op jit(solution)/shard_map/dot_general | solution.py:288
  138.8 26.8 %shard_map.106 = bf16[8,32,4096]{2,1,0:T(8,128)(2,1)} custom-call(bf16[8,32,4096]{2,1,0:T(8,128)(2,1)} %bitcast.22), custom_call_target="tpu_custom_call" | custom-call | tf_op jit(solution)/shard_map/pallas_call | solution.py:106
  165.6 1.9 reduce_sum.72
  167.6 0.5 convolution_convert_fusion.1
  168.0 1.2 reshape.109.x_ref
  169.3 0.0 copy-start.5
  169.3 0.0 copy-start.2
  169.3 32.3 %shard_map.107 = bf16[32,4,4096]{2,1,0:T(4,128)(2,1)} custom-call(bf16[32,4,4096]{2,1,0:T(4,128)(2,1)} %reshape.109.x_ref), custom_call_target="tpu_custom_call" | custom-call | tf_op jit(solution)/shard_map/pallas_call | solution.py:106
  201.6 1.3 reshape.110
  203.0 0.0 copy-done.5
  203.0 0.0 copy-done.2
  203.0 1.8 fusion
  (7 shorter events, 0.1 us)
Async XLA Ops:
  0.0 22.4 %copy-start.1 = (f32[2,4096]{1,0:T(2,128)S(1)}, f32[2,4096]{1,0:T(2,128)}, u32[]{:S(2)}) copy-start(f32[2,4096]{1,0:T(2,128)} %param.14) | copy-start | bytes 98308
  0.0 22.4 %copy-start.6 = (s32[128]{0:T(128)S(1)}, s32[128]{0:T(128)}, u32[]{:S(2)}) copy-start(s32[128]{0:T(128)} %param.11) | copy-start | bytes 1540
  0.0 22.4 %copy-start = (bf16[128,4096]{1,0:T(8,128)(2,1)S(1)}, bf16[128,4096]{1,0:T(8,128)(2,1)}, u32[]{:S(2)}) copy-start(bf16[128,4096]{1,0:T(8,128)(2,1)} %param.10) | copy-start | bytes 3145732
  55.5 2.6 %copy-start.3 = (f32[4096]{0:T(1024)S(1)}, f32[4096]{0:T(1024)}, u32[]{:S(2)}) copy-start(f32[4096]{0:T(1024)} %param.16) | copy-start | bytes 49156
  55.5 2.6 %copy-start.4 = (f32[4096]{0:T(1024)S(1)}, f32[4096]{0:T(1024)}, u32[]{:S(2)}) copy-start(f32[4096]{0:T(1024)} %param.15) | copy-start | bytes 49156
  169.3 33.7 %copy-start.5 = (s32[128]{0:T(128)S(1)}, s32[128]{0:T(128)}, u32[]{:S(2)}) copy-start(s32[128]{0:T(128)} %param.12) | copy-start | bytes 1540
  169.3 33.7 %copy-start.2 = (f32[4096]{0:T(1024)S(1)}, f32[4096]{0:T(1024)}, u32[]{:S(2)}) copy-start(f32[4096]{0:T(1024)} %param.19) | copy-start | bytes 49156

commit v2 on v1

--- a/solution.py
+++ b/solution.py
@@ -46,22 +46,6 @@
 
 def along(axis):
     return lax.axis_size(axis), lambda: lax.axis_index(axis), lambda j: {axis: j}
-
-
-def same_parity():
-    return (
-        lax.axis_size("seq") // 2,
-        lambda: lax.axis_index("seq") // 2,
-        lambda j: {"seq": 2 * j + lax.rem(lax.axis_index("seq"), 2)},
-    )
-
-
-def siblings():
-    return (
-        2,
-        lambda: lax.rem(lax.axis_index("seq"), 2),
-        lambda j: {"seq": lax.axis_index("seq") // 2 * 2 + j},
-    )
 
 
 def exchange(x, group, source, target, out_shape, collective_id):
@@ -115,6 +99,164 @@
         ],
         compiler_params=pltpu.CompilerParams(collective_id=collective_id, has_side_effects=True),
     )(x)
+
+
+def flip(position, bit):
+    return position + bit * (1 - 2 * lax.rem(position // bit, 2))
+
+
+def greet_all(places):
+    barrier = pltpu.get_barrier_semaphore()
+    for place in places:
+        pl.semaphore_signal(barrier, inc=1, device_id={"seq": place}, device_id_type=MESH)
+    pl.semaphore_wait(barrier, len(places))
+
+
+def gather_rows(x, collective_id):
+    rows, width = x.shape
+    half = rows // 2
+
+    def kernel(x_ref, out_ref, send_sem, recv_sem, own_sem):
+        me = lax.axis_index("seq")
+        sibling, left, down = flip(me, 1), flip(me, 2), flip(me, 4)
+        across = flip(left, 4)
+        first, second = pl.ds(0, half), pl.ds(half, half)
+
+        def push(sem, src, dst, place):
+            return pltpu.make_async_remote_copy(
+                src_ref=src,
+                dst_ref=dst,
+                send_sem=send_sem.at[sem],
+                recv_sem=recv_sem.at[sem],
+                device_id={"seq": place},
+                device_id_type=MESH,
+            )
+
+        def own(sem, place):
+            return push(sem, x_ref, out_ref.at[me], place)
+
+        def relay(sem, origin, place):
+            return push(sem, out_ref.at[origin], out_ref.at[origin], place)
+
+        def relay_half(sem, origin, which, place):
+            return push(sem, out_ref.at[origin, which], out_ref.at[origin, which], place)
+
+        greet_all((sibling, left, down))
+        to_left, to_down, to_sibling = own(1, left), own(2, down), own(0, sibling)
+        to_left.start()
+        to_down.start()
+        to_sibling.start()
+        keep = pltpu.make_async_copy(x_ref, out_ref.at[me], own_sem)
+        keep.start()
+        to_left.wait_recv()
+        left_on = relay_half(3, left, first, down)
+        left_on.start()
+        left_over = relay(5, left, sibling)
+        left_over.start()
+        to_down.wait_recv()
+        down_on = relay_half(4, down, second, left)
+        down_on.start()
+        down_over = relay(6, down, sibling)
+        down_over.start()
+        left_on.wait_recv()
+        across_first = relay_half(7, across, first, sibling)
+        across_first.start()
+        down_on.wait_recv()
+        across_second = relay_half(8, across, second, sibling)
+        across_second.start()
+        for copy in (to_sibling, left_over, down_over, across_first, across_second):
+            copy.wait_recv()
+        for copy in (to_left, to_down, to_sibling, left_on, left_over, down_on, down_over, across_first, across_second):
+            copy.wait_send()
+        keep.wait()
+
+    return pl.pallas_call(
+        kernel,
+        out_shape=jax.ShapeDtypeStruct((8, rows, width), x.dtype),
+        in_specs=[pl.BlockSpec(memory_space=pltpu.VMEM)],
+        out_specs=pl.BlockSpec(memory_space=pltpu.VMEM),
+        scratch_shapes=[
+            pltpu.SemaphoreType.DMA((9,)),
+            pltpu.SemaphoreType.DMA((9,)),
+            pltpu.SemaphoreType.DMA,
+        ],
+        compiler_params=pltpu.CompilerParams(collective_id=collective_id, has_side_effects=True),
+    )(x)
+
+
+def scatter_sums(shares, collective_id):
+    _, rows, width = shares.shape
+    half = rows // 2
+
+    def kernel(x_ref, out_ref, near, sums, from_left, from_down, last, passed, send_sem, recv_sem):
+        me = lax.axis_index("seq")
+        sibling, left, down = flip(me, 1), flip(me, 2), flip(me, 4)
+        first, second = pl.ds(0, half), pl.ds(half, half)
+
+        def push(sem, src, dst, place):
+            copy = pltpu.make_async_remote_copy(
+                src_ref=src,
+                dst_ref=dst,
+                send_sem=send_sem.at[sem],
+                recv_sem=recv_sem.at[sem],
+                device_id={"seq": place},
+                device_id_type=MESH,
+            )
+            copy.start()
+            return copy
+
+        def at(place, which):
+            place = flip(place, 2) if which % 2 else place
+            return flip(place, 4) if which // 2 else place
+
+        def wide(value):
+            return value.astype(jnp.float32)
+
+        greet_all((sibling, left, down))
+        order = (3, 1, 2, 0)
+        over = {q: push(q, x_ref.at[at(sibling, q)], near.at[q], sibling) for q in order}
+        for q in order:
+            over[q].wait_recv()
+            sums[q] = (wide(x_ref[at(me, q)]) + wide(near[q])).astype(jnp.bfloat16)
+            if q == 3:
+                left_far = push(4, sums.at[3, first], from_left.at[1], left)
+                down_far = push(5, sums.at[3, second], from_down.at[1], down)
+            if q == 1:
+                left_own = push(6, sums.at[1, first], from_left.at[0], left)
+            if q == 2:
+                down_own = push(7, sums.at[2, second], from_down.at[0], down)
+        left_far.wait_recv()
+        passed[0] = (wide(sums[2, :half]) + wide(from_left[1])).astype(jnp.bfloat16)
+        down_last = push(8, passed.at[0], last.at[0], down)
+        down_far.wait_recv()
+        passed[1] = (wide(sums[1, half:]) + wide(from_down[1])).astype(jnp.bfloat16)
+        left_last = push(9, passed.at[1], last.at[1], left)
+        left_own.wait_recv()
+        down_last.wait_recv()
+        out_ref[:half] = (wide(sums[0, :half]) + wide(from_left[0]) + wide(last[0])).astype(jnp.bfloat16)
+        down_own.wait_recv()
+        left_last.wait_recv()
+        out_ref[half:] = (wide(sums[0, half:]) + wide(from_down[0]) + wide(last[1])).astype(jnp.bfloat16)
+        for copy in (*over.values(), left_far, down_far, left_own, down_own, down_last, left_last):
+            copy.wait_send()
+
+    return pl.pallas_call(
+        kernel,
+        out_shape=jax.ShapeDtypeStruct((rows, width), jnp.bfloat16),
+        in_specs=[pl.BlockSpec(memory_space=pltpu.VMEM)],
+        out_specs=pl.BlockSpec(memory_space=pltpu.VMEM),
+        scratch_shapes=[
+            pltpu.VMEM((4, rows, width), jnp.bfloat16),
+            pltpu.VMEM((4, rows, width), jnp.bfloat16),
+            pltpu.VMEM((2, half, width), jnp.bfloat16),
+            pltpu.VMEM((2, half, width), jnp.bfloat16),
+            pltpu.VMEM((2, half, width), jnp.bfloat16),
+            pltpu.VMEM((2, half, width), jnp.bfloat16),
+            pltpu.SemaphoreType.DMA((10,)),
+            pltpu.SemaphoreType.DMA((10,)),
+        ],
+        compiler_params=pltpu.CompilerParams(collective_id=collective_id, has_side_effects=True),
+    )(shares)
 
 
 def part(ref, j):
@@ -276,7 +418,10 @@
     arriving = exchange(outgoing.reshape(slots), everyone(), part, part, slots, 1)
     balanced = pick(row_of_slot, arriving.reshape(capacity, feature_width), 0)
     normed = layer_norm(balanced, norm_gain, norm_bias)
-    group = exchange(normed, along("seq"), whole, part, (seq_count,) + normed.shape, 2)
+    if seq_count == 8:
+        group = gather_rows(normed, 2)
+    else:
+        group = exchange(normed, along("seq"), whole, part, (seq_count,) + normed.shape, 2)
     group = group.reshape(seq_count * own_rows, feature_width)
     triple = jnp.einsum(
         "rd,tdc->trc", group, qkv_weight, preferred_element_type=jnp.float32
@@ -287,8 +432,11 @@
         attended = attend_by_row(triple)
     shares = jnp.dot(attended, out_weight, preferred_element_type=jnp.float32).astype(jnp.bfloat16)
     shares = shares.reshape(seq_count, own_rows, feature_width)
-    shares = exchange(shares, along("seq"), part, part, shares.shape, 5)
-    projected = jnp.sum(shares.astype(jnp.float32), axis=0).astype(jnp.bfloat16)
+    if seq_count == 8:
+        projected = scatter_sums(shares, 5)
+    else:
+        shares = exchange(shares, along("seq"), part, part, shares.shape, 5)
+        projected = jnp.sum(shares.astype(jnp.float32), axis=0).astype(jnp.bfloat16)
     returning = pick(row_of_slot, projected, 1).astype(jnp.bfloat16)
     returned = exchange(returning.reshape(slots), everyone(), part, part, slots, 6)
     restored = pick(slot_of_token, returned.reshape(capacity, feature_width), 1)

time: 205 us -> 182 us (0.89)
  Pallas kernels: 167 us -> 142 us
    pallas_call x7 -> x5, Pallas kernels: 162 us -> 107 us  [exchange(): pl.pallas_call(kernel, out_shape=jax.ShapeDtypeStruct(out_shape, x.dtype)...]
    pallas_call x0 -> x2, Pallas kernels: none -> 30.9 us  [the longest x1 15.5 us: scatter_sums(): pl.pallas_call(kernel, out_shape=jax.ShapeDtypeStruct((rows, width), jnp....]
where the time goes in v2:
time: 182 us
  Pallas kernels  142 us (78%)
  matrix products  18.6 us (10%)
  other arithmetic  11.4 us (6%)
  local copies, waits for them, and re-layouts  8.9 us (5%)
    pallas_call x5, Pallas kernels, exchange(): pl.pallas_call(kernel, out_shape=jax.ShapeDtypeStruct(out_shape, x.dtype)...  107 us
    pallas_call x1, Pallas kernels, scatter_sums(): pl.pallas_call(kernel, out_shape=jax.ShapeDtypeStruct((rows, width), jnp....  15.5 us
    pallas_call x1, Pallas kernels, gather_rows(): pl.pallas_call(kernel, out_shape=jax.ShapeDtypeStruct((8, rows, width), x...  15.4 us
    dot_general x1, matrix products, local(): jnp.einsum('rd,tdc->trc', group, qkv_weight, preferred_element_type=jnp.f...  9.5 us
    dot_general x1, matrix products, local(): jnp.dot(attended, out_weight, preferred_element_type=jnp.float32)  4.86 us
    pallas_call x1, Pallas kernels, attend(): pl.pallas_call(kernel, grid=(heads, rows // block), out_shape=jax.ShapeDt...  4.69 us
    dot_general x4, matrix products, pick(): lax.dot_general(choice, rows, (((side,), (0,)), ((), ())), preferred_elem...  4.28 us
    sin x1, other arithmetic, position_table(): return jnp.concatenate([jnp.sin(angles), jnp.cos(angles)], axis=1)  3.69 us

profile of v2, /device:TPU:0, one launch (start us, length us, event | category | flops | bytes accessed | tf_op | source)
XLA Modules:
  0.0 181.6 jit_solution(4037713056823930848)
XLA Ops:
  0.0 0.0 copy-start
  0.0 1.4 reduce_sum.54
  1.4 1.1 broadcast_in_dim.113.x_ref
  2.5 0.7 broadcast_compare_fusion
  3.2 0.7 convert_element_type.32
  3.9 0.7 broadcast_compare_fusion.1
  4.5 0.8 select_reduce_fusion
  5.3 11.3 %shard_map.100 = s32[32,1,128]{2,1,0:T(1,128)} custom-call(s32[1,128]{1,0:T(1,128)} %broadcast_in_dim.113.x_ref), custom_call_target="tpu_custom_call" | custom-call | tf_op jit(solution)/shard_map/pallas_call | solution.py:90
  16.6 1.4 slice_reduce_fusion
  18.0 0.6 fusion.10
  18.7 1.3 fusion.13
  20.0 0.1 select_reduce_fusion.1
  20.1 0.1 broadcast_in_dim.121
  20.2 0.1 reshape.104
  20.3 0.1 broadcast_in_dim.120
  20.3 0.1 reshape.103
  20.5 0.9 fusion.17
  21.3 3.7 %multiply_sine_fusion = (f32[128,2048]{1,0:T(8,128)S(1)}, f32[128,2048]{1,0:T(8,128)S(1)}) fusion(f32[2048]{0:T(1024)S(1)} %multiply_exponential_fusion, f32[128]{0:T(128)S(1)} %convert_element_type.32), kind=kLoop, calls=%fused_computation.9 | loop fusion | flops 262144 | bytes 2105856 | tf_op jit(solution)/shard_map/sin | solution.py:21
  25.0 0.0 copy-done
  25.0 0.4 fusion.2
  25.5 0.5 convolution_convert_fusion.2
  26.0 1.2 reshape.105.x_ref
  27.2 30.9 %shard_map.101 = bf16[32,4,4096]{2,1,0:T(4,128)(2,1)} custom-call(bf16[32,4,4096]{2,1,0:T(4,128)(2,1)} %reshape.105.x_ref), custom_call_target="tpu_custom_call" | custom-call | tf_op jit(solution)/shard_map/pallas_call | solution.py:90
  58.1 0.0 copy-start.2
  58.2 0.0 copy-start.3
  58.2 1.3 reshape.106
  59.5 0.5 fusion.18
  60.0 0.2 multiply_reduce_fusion
  60.3 0.0 copy-done.2
  60.3 0.0 copy-done.3
  60.3 0.9 add_convert_fusion.x_ref
  61.2 15.4 %shard_map.102 = bf16[8,32,4096]{2,1,0:T(8,128)(2,1)} custom-call(bf16[32,4096]{1,0:T(8,128)(2,1)} %add_convert_fusion.x_ref), custom_call_target="tpu_custom_call" | custom-call | tf_op jit(solution)/shard_map/pallas_call | solution.py:173
  76.6 9.5 %fusion.3.x_ref = bf16[3,256,512]{2,1,0:T(8,128)(2,1)} fusion(bf16[256,4096,1]{1,0,2:T(8,128)(2,1)} %bitcast.21, bf16[3,4096,512]{2,1,0:T(8,128)(2,1)} %param.17), kind=kOutput, calls=%fused_computation.11 | convolution fusion | flops 3221618688 | bytes 15466496 | tf_op jit(solution)/shard_map/rd,tdc->trc/dot_general | solution.py:426
  86.1 20.5 %shard_map.103 = bf16[3,1024,128]{2,1,0:T(8,128)(2,1)} custom-call(bf16[3,256,512]{2,1,0:T(8,128)(2,1)} %fusion.3.x_ref), custom_call_target="tpu_custom_call" | custom-call | tf_op jit(solution)/shard_map/pallas_call | solution.py:90
  106.6 4.7 %shard_map.104 = bf16[1,1024,128]{2,1,0:T(8,128)(2,1)} custom-call(bf16[3,1,1024,128]{3,2,1,0:T(8,128)(2,1)} %bitcast.18, bf16[3,1,1024,128]{3,2,1,0:T(8,128)(2,1)} %bitcast.19, bf16[3,1,1024,128]{3,2,1,0:T(8,128)(2,1)} %bitcast.20), custom_call_target="tpu_custom_call" | custom-call | tf_op jit(solution)/shard_map/pallas_call | solution.py:287
  111.3 13.7 %shard_map.105 = bf16[256,512]{1,0:T(8,128)(2,1)} custom-call(bf16[1024,128]{1,0:T(8,128)(2,1)} %bitcast.23), custom_call_target="tpu_custom_call" | custom-call | tf_op jit(solution)/shard_map/pallas_call | solution.py:90
  125.1 4.9 %convolution_convert_fusion = bf16[256,4096]{1,0:T(8,128)(2,1)} fusion(bf16[256,512]{1,0:T(8,128)(2,1)} %shard_map.105, bf16[512,4096]{1,0:T(8,128)(2,1)} %param.18), kind=kOutput, calls=%fused_computation | convolution fusion | flops 1074790400 | bytes 6553600 | tf_op jit(solution)/shard_map/dot_general | solution.py:433
  129.9 15.5 %shard_map.106 = bf16[32,4096]{1,0:T(8,128)(2,1)} custom-call(bf16[8,32,4096]{2,1,0:T(8,128)(2,1)} %bitcast.22), custom_call_target="tpu_custom_call" | custom-call | tf_op jit(solution)/shard_map/pallas_call | solution.py:243
  145.4 1.4 convolution_convert_fusion.1
  146.9 1.2 reshape.109.x_ref
  148.1 0.0 copy-start.1
  148.1 30.4 %shard_map.107 = bf16[32,4,4096]{2,1,0:T(4,128)(2,1)} custom-call(bf16[32,4,4096]{2,1,0:T(4,128)(2,1)} %reshape.109.x_ref), custom_call_target="tpu_custom_call" | custom-call | tf_op jit(solution)/shard_map/pallas_call | solution.py:90
  178.5 1.3 reshape.110
  179.8 0.0 copy-done.1
  179.8 1.8 fusion
  (4 shorter events, 0.0 us)
Async XLA Ops:
  0.0 25.0 %copy-start = (bf16[128,4096]{1,0:T(8,128)(2,1)S(1)}, bf16[128,4096]{1,0:T(8,128)(2,1)}, u32[]{:S(2)}) copy-start(bf16[128,4096]{1,0:T(8,128)(2,1)} %param.10) | copy-start | bytes 3145732
  58.1 2.1 %copy-start.2 = (f32[4096]{0:T(1024)S(1)}, f32[4096]{0:T(1024)}, u32[]{:S(2)}) copy-start(f32[4096]{0:T(1024)} %param.16) | copy-start | bytes 49156
  58.2 2.1 %copy-start.3 = (f32[4096]{0:T(1024)S(1)}, f32[4096]{0:T(1024)}, u32[]{:S(2)}) copy-start(f32[4096]{0:T(1024)} %param.15) | copy-start | bytes 49156
  148.1 31.7 %copy-start.1 = (f32[4096]{0:T(1024)S(1)}, f32[4096]{0:T(1024)}, u32[]{:S(2)}) copy-start(f32[4096]{0:T(1024)} %param.19) | copy-start | bytes 49156

commit v3 on v1

--- a/solution.py
+++ b/solution.py
@@ -46,22 +46,6 @@
 
 def along(axis):
     return lax.axis_size(axis), lambda: lax.axis_index(axis), lambda j: {axis: j}
-
-
-def same_parity():
-    return (
-        lax.axis_size("seq") // 2,
-        lambda: lax.axis_index("seq") // 2,
-        lambda j: {"seq": 2 * j + lax.rem(lax.axis_index("seq"), 2)},
-    )
-
-
-def siblings():
-    return (
-        2,
-        lambda: lax.rem(lax.axis_index("seq"), 2),
-        lambda j: {"seq": lax.axis_index("seq") // 2 * 2 + j},
-    )
 
 
 def exchange(x, group, source, target, out_shape, collective_id):
@@ -115,6 +99,322 @@
         ],
         compiler_params=pltpu.CompilerParams(collective_id=collective_id, has_side_effects=True),
     )(x)
+
+
+CHUNKS = 4
+
+
+def remote(src, dst, sems, at, device):
+    send_sem, recv_sem = sems
+    return pltpu.make_async_remote_copy(
+        src_ref=src,
+        dst_ref=dst,
+        send_sem=send_sem.at[at],
+        recv_sem=recv_sem.at[at],
+        device_id=device,
+        device_id_type=MESH,
+    )
+
+
+def aligned(start, size):
+    return pl.ds(pl.multiple_of(start * size, size), size)
+
+
+def greet_line_and_plane(seq_count, ctx_count):
+    me, level = lax.axis_index("seq"), lax.axis_index("ctx")
+    barrier = pltpu.get_barrier_semaphore()
+    for step in range(1, seq_count):
+        peer = {"seq": lax.rem(me + step, seq_count)}
+        pl.semaphore_signal(barrier, inc=1, device_id=peer, device_id_type=MESH)
+    for step in range(1, ctx_count):
+        peer = {"ctx": lax.rem(level + step, ctx_count)}
+        pl.semaphore_signal(barrier, inc=1, device_id=peer, device_id_type=MESH)
+    pl.semaphore_wait(barrier, seq_count + ctx_count - 2)
+
+
+def regrouping(capacity, outer, inner, slot_count):
+    row = lax.broadcasted_iota(jnp.int32, (capacity, capacity), 0)
+    column = lax.broadcasted_iota(jnp.int32, (capacity, capacity), 1)
+    first = row // (inner * slot_count)
+    second = row // slot_count % inner
+    wanted = (second * outer + first) * slot_count + row % slot_count
+    return (column == wanted).astype(jnp.bfloat16)
+
+
+def moved(choice, rows):
+    return jnp.dot(choice, rows, preferred_element_type=jnp.float32).astype(jnp.bfloat16)
+
+
+def spread_rows(outgoing, choice, slot_count, collective_id):
+    capacity, width = outgoing.shape
+    rows = choice.shape[0]
+    half = rows // 2
+    seq_count, ctx_count = lax.axis_size("seq"), lax.axis_size("ctx")
+    line_rows, plane_rows = capacity // ctx_count, capacity // seq_count
+    part_width = width // CHUNKS
+
+    def kernel(x_ref, choice_ref, out_ref, mid, ordered, arrived, zs, zr, ps, pr, gs, gr, own_sem, own_sems):
+        me, level = lax.axis_index("seq"), lax.axis_index("ctx")
+        sibling, left, down = flip(me, 1), flip(me, 2), flip(me, 4)
+        across = flip(left, 4)
+        all_rows, first, second = pl.ds(0, rows), pl.ds(0, half), pl.ds(half, half)
+        along_line, over_plane, gathering = (zs, zr), (ps, pr), (gs, gr)
+
+        def cols(k):
+            return pl.ds(k * part_width, part_width)
+
+        def line(k, step):
+            peer = lax.rem(level + step, ctx_count)
+            src = x_ref.at[aligned(peer, line_rows), cols(k)]
+            dst = mid.at[aligned(level, line_rows), cols(k)]
+            return remote(src, dst, along_line, (k, step), {"ctx": peer})
+
+        def plane(k, step):
+            peer = lax.rem(me + step, seq_count)
+            src = ordered.at[aligned(peer, plane_rows), cols(k)]
+            dst = arrived.at[aligned(me, plane_rows), cols(k)]
+            return remote(src, dst, over_plane, (k, step), {"seq": peer})
+
+        def plane_own(k):
+            here = aligned(me, plane_rows)
+            return pltpu.make_async_copy(ordered.at[here, cols(k)], arrived.at[here, cols(k)], own_sems.at[k])
+
+        moves = (
+            (me, all_rows, sibling),
+            (me, all_rows, left),
+            (me, all_rows, down),
+            (left, first, down),
+            (down, second, left),
+            (left, all_rows, sibling),
+            (down, all_rows, sibling),
+            (across, first, sibling),
+            (across, second, sibling),
+        )
+
+        def hand(k, at):
+            origin, which, place = moves[at]
+            ref = out_ref.at[origin, which, cols(k)]
+            return remote(ref, ref, gathering, (k, at), {"seq": place})
+
+        greet_line_and_plane(seq_count, ctx_count)
+        for k in range(CHUNKS):
+            for step in range(1, ctx_count):
+                line(k, step).start()
+        here = aligned(level, line_rows)
+        own = pltpu.make_async_copy(x_ref.at[here], mid.at[here], own_sem)
+        own.start()
+        regroup = regrouping(capacity, seq_count, ctx_count, slot_count)
+        own.wait()
+        for turn in range(CHUNKS + 3):
+            k = turn - 3
+            if 0 <= k < CHUNKS:
+                hand(k, 3).wait_recv()
+                hand(k, 7).start()
+                hand(k, 4).wait_recv()
+                hand(k, 8).start()
+            k = turn - 2
+            if 0 <= k < CHUNKS:
+                hand(k, 1).wait_recv()
+                hand(k, 3).start()
+                hand(k, 5).start()
+                hand(k, 2).wait_recv()
+                hand(k, 4).start()
+                hand(k, 6).start()
+            k = turn - 1
+            if 0 <= k < CHUNKS:
+                for step in range(1, seq_count):
+                    plane(k, step).wait_recv()
+                plane_own(k).wait()
+                out_ref[me, :, cols(k)] = moved(choice_ref[...], arrived[:, cols(k)])
+                for at in (1, 2, 0):
+                    hand(k, at).start()
+            k = turn
+            if k < CHUNKS:
+                for step in range(1, ctx_count):
+                    line(k, step).wait_recv()
+                ordered[:, cols(k)] = moved(regroup, mid[:, cols(k)])
+                for step in range(1, seq_count):
+                    plane(k, step).start()
+                plane_own(k).start()
+        for k in range(CHUNKS):
+            for at in (0, 5, 6, 7, 8):
+                hand(k, at).wait_recv()
+            for at in range(9):
+                hand(k, at).wait_send()
+            for step in range(1, seq_count):
+                plane(k, step).wait_send()
+            for step in range(1, ctx_count):
+                line(k, step).wait_send()
+
+    dma = pltpu.SemaphoreType.DMA
+    return pl.pallas_call(
+        kernel,
+        out_shape=jax.ShapeDtypeStruct((seq_count, rows, width), jnp.bfloat16),
+        in_specs=[pl.BlockSpec(memory_space=pltpu.VMEM)] * 2,
+        out_specs=pl.BlockSpec(memory_space=pltpu.VMEM),
+        scratch_shapes=[pltpu.VMEM((capacity, width), jnp.bfloat16)] * 3
+        + [dma((CHUNKS, ctx_count))] * 2
+        + [dma((CHUNKS, seq_count))] * 2
+        + [dma((CHUNKS, 9))] * 2
+        + [dma, dma((CHUNKS,))],
+        compiler_params=pltpu.CompilerParams(collective_id=collective_id, has_side_effects=True),
+    )(outgoing, choice)
+
+
+def flip(position, bit):
+    return position + bit * (1 - 2 * lax.rem(position // bit, 2))
+
+
+def return_rows(attended, out_weight, choice, slot_count, collective_id):
+    width = out_weight.shape[1]
+    capacity, rows = choice.shape
+    half = rows // 2
+    seq_count, ctx_count = lax.axis_size("seq"), lax.axis_size("ctx")
+    line_rows, plane_rows = capacity // ctx_count, capacity // seq_count
+    part_width = width // CHUNKS
+
+    def kernel(
+        x_ref, w_ref, choice_ref, out_ref, shares, near, sums, from_left, from_down, last, passed, total,
+        sorted_rows, arrived, ordered, ss, sr, ps, pr, zs, zr, own_sems, line_sems,
+    ):
+        me, level = lax.axis_index("seq"), lax.axis_index("ctx")
+        sibling, left, down = flip(me, 1), flip(me, 2), flip(me, 4)
+        first, second = pl.ds(0, half), pl.ds(half, half)
+        summing, over_plane, along_line = (ss, sr), (ps, pr), (zs, zr)
+
+        def cols(k):
+            return pl.ds(k * part_width, part_width)
+
+        def at(place, which):
+            place = flip(place, 2) if which % 2 else place
+            return flip(place, 4) if which // 2 else place
+
+        def over(k, q):
+            src = shares.at[aligned(at(sibling, q), rows), cols(k)]
+            return remote(src, near.at[q, :, cols(k)], summing, (k, q), {"seq": sibling})
+
+        def far(k, which):
+            if which == 0:
+                return remote(sums.at[3, first, cols(k)], from_left.at[1, :, cols(k)], summing, (k, 4), {"seq": left})
+            if which == 1:
+                return remote(sums.at[3, second, cols(k)], from_down.at[1, :, cols(k)], summing, (k, 5), {"seq": down})
+            if which == 2:
+                return remote(sums.at[1, first, cols(k)], from_left.at[0, :, cols(k)], summing, (k, 6), {"seq": left})
+            if which == 3:
+                return remote(sums.at[2, second, cols(k)], from_down.at[0, :, cols(k)], summing, (k, 7), {"seq": down})
+            if which == 4:
+                return remote(passed.at[0, :, cols(k)], last.at[0, :, cols(k)], summing, (k, 8), {"seq": down})
+            return remote(passed.at[1, :, cols(k)], last.at[1, :, cols(k)], summing, (k, 9), {"seq": left})
+
+        def plane(k, step):
+            peer = lax.rem(me + step, seq_count)
+            src = sorted_rows.at[aligned(peer, plane_rows), cols(k)]
+            dst = arrived.at[aligned(me, plane_rows), cols(k)]
+            return remote(src, dst, over_plane, (k, step), {"seq": peer})
+
+        def plane_own(k):
+            here = aligned(me, plane_rows)
+            return pltpu.make_async_copy(sorted_rows.at[here, cols(k)], arrived.at[here, cols(k)], own_sems.at[k])
+
+        def line(k, step):
+            peer = lax.rem(level + step, ctx_count)
+            src = ordered.at[aligned(peer, line_rows), cols(k)]
+            dst = out_ref.at[aligned(level, line_rows), cols(k)]
+            return remote(src, dst, along_line, (k, step), {"ctx": peer})
+
+        def line_own(k):
+            here = aligned(level, line_rows)
+            return pltpu.make_async_copy(ordered.at[here, cols(k)], out_ref.at[here, cols(k)], line_sems.at[k])
+
+        def wide(value):
+            return value.astype(jnp.float32)
+
+        def narrow(value):
+            return value.astype(jnp.bfloat16)
+
+        greet_line_and_plane(seq_count, ctx_count)
+        regroup = regrouping(capacity, ctx_count, seq_count, slot_count)
+        order = (3, 1, 2, 0)
+        for turn in range(CHUNKS + 4):
+            k = turn - 4
+            if 0 <= k < CHUNKS:
+                for step in range(1, seq_count):
+                    plane(k, step).wait_recv()
+                plane_own(k).wait()
+                ordered[:, cols(k)] = moved(regroup, arrived[:, cols(k)])
+                for step in range(1, ctx_count):
+                    line(k, step).start()
+                line_own(k).start()
+            k = turn - 3
+            if 0 <= k < CHUNKS:
+                c = cols(k)
+                far(k, 2).wait_recv()
+                far(k, 4).wait_recv()
+                total[:half, c] = narrow(wide(sums[0, :half, c]) + wide(from_left[0, :, c]) + wide(last[0, :, c]))
+                far(k, 3).wait_recv()
+                far(k, 5).wait_recv()
+                total[half:, c] = narrow(wide(sums[0, half:, c]) + wide(from_down[0, :, c]) + wide(last[1, :, c]))
+                sorted_rows[:, c] = moved(choice_ref[...], total[:, c])
+                for step in range(1, seq_count):
+                    plane(k, step).start()
+                plane_own(k).start()
+            k = turn - 2
+            if 0 <= k < CHUNKS:
+                c = cols(k)
+                far(k, 0).wait_recv()
+                passed[0, :, c] = narrow(wide(sums[2, :half, c]) + wide(from_left[1, :, c]))
+                far(k, 4).start()
+                far(k, 1).wait_recv()
+                passed[1, :, c] = narrow(wide(sums[1, half:, c]) + wide(from_down[1, :, c]))
+                far(k, 5).start()
+            k = turn - 1
+            if 0 <= k < CHUNKS:
+                c = cols(k)
+                for q in order:
+                    over(k, q).wait_recv()
+                    mine = shares[aligned(at(me, q), rows), c]
+                    sums[q, :, c] = narrow(wide(mine) + wide(near[q, :, c]))
+                    if q == 3:
+                        far(k, 0).start()
+                        far(k, 1).start()
+                    if q == 1:
+                        far(k, 2).start()
+                    if q == 2:
+                        far(k, 3).start()
+            k = turn
+            if k < CHUNKS:
+                shares[:, cols(k)] = moved(x_ref[...], w_ref[:, cols(k)])
+                for q in order:
+                    over(k, q).start()
+        for k in range(CHUNKS):
+            for step in range(1, ctx_count):
+                line(k, step).wait()
+            line_own(k).wait()
+            for step in range(1, seq_count):
+                plane(k, step).wait_send()
+            for q in order:
+                over(k, q).wait_send()
+            for which in range(6):
+                far(k, which).wait_send()
+
+    dma = pltpu.SemaphoreType.DMA
+    bf16 = jnp.bfloat16
+    return pl.pallas_call(
+        kernel,
+        out_shape=jax.ShapeDtypeStruct((capacity, width), bf16),
+        in_specs=[pl.BlockSpec(memory_space=pltpu.VMEM)] * 3,
+        out_specs=pl.BlockSpec(memory_space=pltpu.VMEM),
+        scratch_shapes=[pltpu.VMEM((seq_count * rows, width), bf16)]
+        + [pltpu.VMEM((4, rows, width), bf16)] * 2
+        + [pltpu.VMEM((2, half, width), bf16)] * 4
+        + [pltpu.VMEM((rows, width), bf16)]
+        + [pltpu.VMEM((capacity, width), bf16)] * 3
+        + [dma((CHUNKS, 10))] * 2
+        + [dma((CHUNKS, seq_count))] * 2
+        + [dma((CHUNKS, ctx_count))] * 2
+        + [dma((CHUNKS,))] * 2,
+        compiler_params=pltpu.CompilerParams(collective_id=collective_id, has_side_effects=True),
+    )(attended, out_weight, choice)
 
 
 def part(ref, j):
@@ -249,9 +549,11 @@
         jnp.sum(jnp.where(token_index[None, :] <= token_index[:, None], keep_mask[None, :], 0), axis=1) - 1
     )
     global_rank = my_start + local_rank
-    token_slot = jnp.where(
-        visible, global_rank % devices * slot_count + local_rank // devices, capacity
-    )
+    owner = global_rank % devices
+    piped = seq_count == 8 and slot_count * ctx_count % 16 == 0
+    if piped:
+        owner = owner % ctx_count * seq_count + owner // ctx_count
+    token_slot = jnp.where(visible, owner * slot_count + local_rank // devices, capacity)
     slot_index = jnp.arange(capacity, dtype=jnp.int32)
     slot_of_token = (token_slot[:, None] == slot_index[None, :]).astype(jnp.bfloat16)
     slot_place = slot_index % slot_count
@@ -271,12 +573,15 @@
             choice, rows, (((side,), (0,)), ((), ())), preferred_element_type=jnp.float32
         )
 
-    outgoing = pick(slot_of_token, embedded, 0).astype(jnp.bfloat16)
+    normed = layer_norm(embedded, norm_gain, norm_bias)
+    outgoing = pick(slot_of_token, normed, 0).astype(jnp.bfloat16)
     slots = (devices, slot_count, feature_width)
-    arriving = exchange(outgoing.reshape(slots), everyone(), part, part, slots, 1)
-    balanced = pick(row_of_slot, arriving.reshape(capacity, feature_width), 0)
-    normed = layer_norm(balanced, norm_gain, norm_bias)
-    group = exchange(normed, along("seq"), whole, part, (seq_count,) + normed.shape, 2)
+    if piped:
+        group = spread_rows(outgoing, row_of_slot.T, slot_count, 1)
+    else:
+        arriving = exchange(outgoing.reshape(slots), everyone(), part, part, slots, 1)
+        own_normed = pick(row_of_slot, arriving.reshape(capacity, feature_width), 0).astype(jnp.bfloat16)
+        group = exchange(own_normed, along("seq"), whole, part, (seq_count,) + own_normed.shape, 2)
     group = group.reshape(seq_count * own_rows, feature_width)
     triple = jnp.einsum(
         "rd,tdc->trc", group, qkv_weight, preferred_element_type=jnp.float32
@@ -285,13 +590,17 @@
         attended = attend_by_head(triple)
     else:
         attended = attend_by_row(triple)
-    shares = jnp.dot(attended, out_weight, preferred_element_type=jnp.float32).astype(jnp.bfloat16)
-    shares = shares.reshape(seq_count, own_rows, feature_width)
-    shares = exchange(shares, along("seq"), part, part, shares.shape, 5)
-    projected = jnp.sum(shares.astype(jnp.float32), axis=0).astype(jnp.bfloat16)
-    returning = pick(row_of_slot, projected, 1).astype(jnp.bfloat16)
-    returned = exchange(returning.reshape(slots), everyone(), part, part, slots, 6)
-    restored = pick(slot_of_token, returned.reshape(capacity, feature_width), 1)
+    if piped:
+        returned = return_rows(attended, out_weight, row_of_slot, slot_count, 5)
+    else:
+        shares = jnp.dot(attended, out_weight, preferred_element_type=jnp.float32).astype(jnp.bfloat16)
+        shares = shares.reshape(seq_count, own_rows, feature_width)
+        shares = exchange(shares, along("seq"), part, part, shares.shape, 5)
+        projected = jnp.sum(shares.astype(jnp.float32), axis=0).astype(jnp.bfloat16)
+        returning = pick(row_of_slot, projected, 1).astype(jnp.bfloat16)
+        returned = exchange(returning.reshape(slots), everyone(), part, part, slots, 6)
+        returned = returned.reshape(capacity, feature_width)
+    restored = pick(slot_of_token, returned, 1)
     return jnp.where(visible[:, None], embedded.astype(jnp.float32) + restored, mask_token[None, :])
 
 

time: 205 us -> 171 us (0.83)
  Pallas kernels: 167 us -> 144 us
  local copies, waits for them, and re-layouts: 8.08 us -> 2.97 us
  matrix products: 17.7 us -> 14.2 us
  other arithmetic: 12.1 us -> 9.04 us
    pallas_call x7 -> x3, Pallas kernels: 162 us -> 45.6 us  [exchange(): pl.pallas_call(kernel, out_shape=jax.ShapeDtypeStruct(out_shape, x.dtype)...]
    pallas_call x0 -> x2, Pallas kernels: none -> 94.1 us  [the longest x1 49.4 us: spread_rows(): pl.pallas_call(kernel, out_shape=jax.ShapeDtypeStruct((seq_count, rows, w...]
    reshape x4 -> x0, local copies, waits for them, and re-layouts: 5.11 us -> none  [the longest x1 1.35 us: local(): balanced = pick(row_of_slot, arriving.reshape(capacity, feature_width), 0)]
    dot_general x1 -> x0, matrix products: 4.86 us -> none  [local(): jnp.dot(attended, out_weight, preferred_element_type=jnp.float32)]
    dot_general x4 -> x2, matrix products: 3.33 us -> 4.72 us  [pick(): lax.dot_general(choice, rows, (((side,), (0,)), ((), ())), preferred_elem...]
where the time goes in v3:
time: 171 us
  Pallas kernels  144 us (84%)
  matrix products  14.2 us (8%)
  other arithmetic  9.04 us (5%)
  local copies, waits for them, and re-layouts  2.97 us (2%)
    pallas_call x1, Pallas kernels, spread_rows(): pl.pallas_call(kernel, out_shape=jax.ShapeDtypeStruct((seq_count, rows, w...  49.4 us
    pallas_call x3, Pallas kernels, exchange(): pl.pallas_call(kernel, out_shape=jax.ShapeDtypeStruct(out_shape, x.dtype)...  45.6 us
    pallas_call x1, Pallas kernels, return_rows(): pl.pallas_call(kernel, out_shape=jax.ShapeDtypeStruct((capacity, width),...  44.7 us
    dot_general x1, matrix products, local(): jnp.einsum('rd,tdc->trc', group, qkv_weight, preferred_element_type=jnp.f...  9.5 us
    dot_general x2, matrix products, pick(): lax.dot_general(choice, rows, (((side,), (0,)), ((), ())), preferred_elem...  4.72 us
    pallas_call x1, Pallas kernels, attend(): pl.pallas_call(kernel, grid=(heads, rows // block), out_shape=jax.ShapeDt...  4.69 us
    sin x1, other arithmetic, position_table(): return jnp.concatenate([jnp.sin(angles), jnp.cos(angles)], axis=1)  3.69 us

profile of v3, /device:TPU:0, one launch (start us, length us, event | category | flops | bytes accessed | tf_op | source)
XLA Modules:
  0.0 170.7 jit_solution(11908008153876652291)
XLA Ops:
  0.0 0.0 copy-start.1
  0.0 0.0 copy-start.6
  0.0 0.0 copy-start
  0.0 0.8 convert_element_type.31
  0.8 3.7 %multiply_sine_fusion = (f32[128,2048]{1,0:T(8,128)S(1)}, f32[128,2048]{1,0:T(8,128)S(1)}) fusion(f32[2048]{0:T(1024)S(1)} %multiply_exponential_fusion, f32[128]{0:T(128)S(1)} %convert_element_type.31), kind=kLoop, calls=%fused_computation.15 | loop fusion | flops 262144 | bytes 2105856 | tf_op jit(solution)/shard_map/sin | solution.py:21
  4.5 0.0 copy-done.1
  4.5 0.0 copy-done.6
  4.5 0.0 copy-done
  4.5 0.0 copy-start.3
  4.6 0.0 copy-start.4
  4.6 0.0 copy-start.5
  4.6 0.6 convert_reduce_fusion
  5.2 0.4 fusion.3
  5.7 0.0 copy-done.3
  5.7 0.6 reduce_sum.54
  6.3 1.1 broadcast_in_dim.113.x_ref
  7.5 11.3 %shard_map.100 = s32[32,1,128]{2,1,0:T(1,128)} custom-call(s32[1,128]{1,0:T(1,128)} %broadcast_in_dim.113.x_ref), custom_call_target="tpu_custom_call" | custom-call | tf_op jit(solution)/shard_map/pallas_call | solution.py:90
  18.8 1.4 slice_reduce_fusion
  20.2 0.6 fusion.20
  20.9 0.1 select_reduce_fusion
  21.0 0.7 add_select_fusion
  21.6 0.0 copy-done.4
  21.6 0.0 copy-done.5
  21.7 1.7 convolution_convert_fusion.x_ref
  23.3 0.1 select_reduce_fusion.1
  23.4 0.1 broadcast_in_dim.120
  23.5 0.1 reshape.88
  23.6 0.1 broadcast_in_dim.121
  23.7 0.1 reshape.89
  23.8 0.6 fusion.18.choice_ref
  24.4 49.4 %shard_map.101 = bf16[8,32,4096]{2,1,0:T(8,128)(2,1)} custom-call(bf16[128,4096]{1,0:T(8,128)(2,1)} %convolution_convert_fusion.x_ref, bf16[32,128]{1,0:T(8,128)(2,1)} %fusion.18.choice_ref), custom_call_target="tpu_custom_call" | custom-call | tf_op jit(solution)/shard_map/pallas_call | solution.py:250
  73.8 9.5 %fusion.9.x_ref = bf16[3,256,512]{2,1,0:T(8,128)(2,1)} fusion(bf16[256,4096,1]{1,0,2:T(8,128)(2,1)} %bitcast.15, bf16[3,4096,512]{2,1,0:T(8,128)(2,1)} %param.17), kind=kOutput, calls=%fused_computation.17 | convolution fusion | flops 3221618688 | bytes 15466496 | tf_op jit(solution)/shard_map/rd,tdc->trc/dot_general | solution.py:586
  83.3 21.5 %shard_map.102 = bf16[3,1024,128]{2,1,0:T(8,128)(2,1)} custom-call(bf16[3,256,512]{2,1,0:T(8,128)(2,1)} %fusion.9.x_ref), custom_call_target="tpu_custom_call" | custom-call | tf_op jit(solution)/shard_map/pallas_call | solution.py:90
  104.9 4.7 %shard_map.103 = bf16[1,1024,128]{2,1,0:T(8,128)(2,1)} custom-call(bf16[3,1,1024,128]{3,2,1,0:T(8,128)(2,1)} %bitcast.12, bf16[3,1,1024,128]{3,2,1,0:T(8,128)(2,1)} %bitcast.13, bf16[3,1,1024,128]{3,2,1,0:T(8,128)(2,1)} %bitcast.14), custom_call_target="tpu_custom_call" | custom-call | tf_op jit(solution)/shard_map/pallas_call | solution.py:445
  109.6 12.7 %shard_map.104.x_ref = bf16[256,512]{1,0:T(8,128)(2,1)} custom-call(bf16[1024,128]{1,0:T(8,128)(2,1)} %bitcast.16), custom_call_target="tpu_custom_call" | custom-call | tf_op jit(solution)/shard_map/pallas_call | solution.py:90
  122.3 0.7 fusion.15.choice_ref
  123.0 0.0 copy-start.2
  123.0 44.7 %shard_map.105 = bf16[128,4096]{1,0:T(8,128)(2,1)} custom-call(bf16[256,512]{1,0:T(8,128)(2,1)} %shard_map.104.x_ref, bf16[512,4096]{1,0:T(8,128)(2,1)} %w_ref.1, bf16[128,32]{1,0:T(8,128)(2,1)} %fusion.15.choice_ref), custom_call_target="tpu_custom_call" | custom-call | tf_op jit(solution)/shard_map/pallas_call | solution.py:402
  167.7 0.0 copy-done.2
  167.7 3.0 %fusion = f32[128,4096]{1,0:T(8,128)} fusion(bf16[128,4096]{1,0:T(8,128)(2,1)} %shard_map.105, bf16[128,4096]{1,0:T(8,128)(2,1)S(1)} %get-tuple-element.6, f32[4096]{0:T(1024)S(1)} %copy-done.2, pred[128]{0:T(512)(128)(4,1)S(1)} %broadcast_compare_fusion.1, s32[128]{0:T(128)S(1)} %add_select_fusion), kind=kOutput, calls=%fused_computation.1 | convolution fusion | flops 135806976 | bytes 4211328 | tf_op jit(solution)/shard_map/dot_general | solution.py:572
  (7 shorter events, 0.1 us)
Async XLA Ops:
  0.0 4.5 %copy-start.1 = (f32[2,4096]{1,0:T(2,128)S(1)}, f32[2,4096]{1,0:T(2,128)}, u32[]{:S(2)}) copy-start(f32[2,4096]{1,0:T(2,128)} %param.14) | copy-start | bytes 98308
  0.0 4.5 %copy-start.6 = (s32[128]{0:T(128)S(1)}, s32[128]{0:T(128)}, u32[]{:S(2)}) copy-start(s32[128]{0:T(128)} %param.11) | copy-start | bytes 1540
  0.0 4.5 %copy-start = (bf16[128,4096]{1,0:T(8,128)(2,1)S(1)}, bf16[128,4096]{1,0:T(8,128)(2,1)}, u32[]{:S(2)}) copy-start(bf16[128,4096]{1,0:T(8,128)(2,1)} %param.10) | copy-start | bytes 3145732
  4.5 1.1 copy-start.3
  4.6 17.1 %copy-start.4 = (f32[4096]{0:T(1024)S(1)}, f32[4096]{0:T(1024)}, u32[]{:S(2)}) copy-start(f32[4096]{0:T(1024)} %param.16) | copy-start | bytes 49156
  4.6 17.1 %copy-start.5 = (f32[4096]{0:T(1024)S(1)}, f32[4096]{0:T(1024)}, u32[]{:S(2)}) copy-start(f32[4096]{0:T(1024)} %param.15) | copy-start | bytes 49156
  123.0 44.7 %copy-start.2 = (f32[4096]{0:T(1024)S(1)}, f32[4096]{0:T(1024)}, u32[]{:S(2)}) copy-start(f32[4096]{0:T(1024)} %param.19) | copy-start | bytes 49156

commit v4 on v3

--- a/solution.py
+++ b/solution.py
@@ -145,7 +145,7 @@
     return jnp.dot(choice, rows, preferred_element_type=jnp.float32).astype(jnp.bfloat16)
 
 
-def spread_rows(outgoing, choice, slot_count, collective_id):
+def spread_rows(outgoing, choice, qkv_weight, slot_count, collective_id):
     capacity, width = outgoing.shape
     rows = choice.shape[0]
     half = rows // 2
@@ -153,7 +153,12 @@
     line_rows, plane_rows = capacity // ctx_count, capacity // seq_count
     part_width = width // CHUNKS
 
-    def kernel(x_ref, choice_ref, out_ref, mid, ordered, arrived, zs, zr, ps, pr, gs, gr, own_sem, own_sems):
+    kinds, _, local_width = qkv_weight.shape
+
+    def kernel(
+        x_ref, choice_ref, w_hbm, triple_ref, mid, ordered, arrived, out_ref, w_ref, total,
+        zs, zr, ps, pr, gs, gr, own_sem, own_sems, w_sems,
+    ):
         me, level = lax.axis_index("seq"), lax.axis_index("ctx")
         sibling, left, down = flip(me, 1), flip(me, 2), flip(me, 4)
         across = flip(left, 4)
@@ -196,16 +201,35 @@
             ref = out_ref.at[origin, which, cols(k)]
             return remote(ref, ref, gathering, (k, at), {"seq": place})
 
+        def fetch(k):
+            return pltpu.make_async_copy(w_hbm.at[:, cols(k), :], w_ref.at[:, cols(k), :], w_sems.at[k])
+
         greet_line_and_plane(seq_count, ctx_count)
         for k in range(CHUNKS):
             for step in range(1, ctx_count):
                 line(k, step).start()
+        for k in range(CHUNKS):
+            fetch(k).start()
         here = aligned(level, line_rows)
         own = pltpu.make_async_copy(x_ref.at[here], mid.at[here], own_sem)
         own.start()
         regroup = regrouping(capacity, seq_count, ctx_count, slot_count)
         own.wait()
-        for turn in range(CHUNKS + 3):
+        for turn in range(CHUNKS + 4):
+            k = turn - 4
+            if 0 <= k < CHUNKS:
+                for at in (0, 5, 6, 7, 8):
+                    hand(k, at).wait_recv()
+                fetch(k).wait()
+                gathered = out_ref[:, :, cols(k)].reshape(seq_count * rows, part_width)
+                for kind in range(kinds):
+                    term = jnp.dot(gathered, w_ref[kind, cols(k), :], preferred_element_type=jnp.float32)
+                    if k == 0:
+                        total[kind] = term
+                    elif k < CHUNKS - 1:
+                        total[kind] += term
+                    else:
+                        triple_ref[kind] = (total[kind] + term).astype(jnp.bfloat16)
             k = turn - 3
             if 0 <= k < CHUNKS:
                 hand(k, 3).wait_recv()
@@ -237,8 +261,6 @@
                     plane(k, step).start()
                 plane_own(k).start()
         for k in range(CHUNKS):
-            for at in (0, 5, 6, 7, 8):
-                hand(k, at).wait_recv()
             for at in range(9):
                 hand(k, at).wait_send()
             for step in range(1, seq_count):
@@ -249,16 +271,21 @@
     dma = pltpu.SemaphoreType.DMA
     return pl.pallas_call(
         kernel,
-        out_shape=jax.ShapeDtypeStruct((seq_count, rows, width), jnp.bfloat16),
-        in_specs=[pl.BlockSpec(memory_space=pltpu.VMEM)] * 2,
+        out_shape=jax.ShapeDtypeStruct((kinds, seq_count * rows, local_width), jnp.bfloat16),
+        in_specs=[pl.BlockSpec(memory_space=pltpu.VMEM)] * 2 + [pl.BlockSpec(memory_space=pl.ANY)],
         out_specs=pl.BlockSpec(memory_space=pltpu.VMEM),
         scratch_shapes=[pltpu.VMEM((capacity, width), jnp.bfloat16)] * 3
+        + [
+            pltpu.VMEM((seq_count, rows, width), jnp.bfloat16),
+            pltpu.VMEM(qkv_weight.shape, jnp.bfloat16),
+            pltpu.VMEM((kinds, seq_count * rows, local_width), jnp.float32),
+        ]
         + [dma((CHUNKS, ctx_count))] * 2
         + [dma((CHUNKS, seq_count))] * 2
         + [dma((CHUNKS, 9))] * 2
-        + [dma, dma((CHUNKS,))],
+        + [dma, dma((CHUNKS,)), dma((CHUNKS,))],
         compiler_params=pltpu.CompilerParams(collective_id=collective_id, has_side_effects=True),
-    )(outgoing, choice)
+    )(outgoing, choice, qkv_weight)
 
 
 def flip(position, bit):
@@ -577,15 +604,17 @@
     outgoing = pick(slot_of_token, normed, 0).astype(jnp.bfloat16)
     slots = (devices, slot_count, feature_width)
     if piped:
-        group = spread_rows(outgoing, row_of_slot.T, slot_count, 1)
+        triple = spread_rows(outgoing, row_of_slot.T, qkv_weight, slot_count, 1)
     else:
         arriving = exchange(outgoing.reshape(slots), everyone(), part, part, slots, 1)
         own_normed = pick(row_of_slot, arriving.reshape(capacity, feature_width), 0).astype(jnp.bfloat16)
         group = exchange(own_normed, along("seq"), whole, part, (seq_count,) + own_normed.shape, 2)
-    group = group.reshape(seq_count * own_rows, feature_width)
-    triple = jnp.einsum(
-        "rd,tdc->trc", group, qkv_weight, preferred_element_type=jnp.float32
-    ).astype(jnp.bfloat16)
+        triple = jnp.einsum(
+            "rd,tdc->trc",
+            group.reshape(seq_count * own_rows, feature_width),
+            qkv_weight,
+            preferred_element_type=jnp.float32,
+        ).astype(jnp.bfloat16)
     if triple.shape[2] % (ctx_count * HEAD_DIM) == 0:
         attended = attend_by_head(triple)
     else:

time: 171 us -> 167 us (0.977)
  matrix products: 14.2 us -> 4.73 us
  other arithmetic: 9.04 us -> 12.3 us
    dot_general x1 -> x0, matrix products: 9.5 us -> none  [local(): jnp.einsum('rd,tdc->trc', group, qkv_weight, preferred_element_type=jnp.f...]
where the time goes in v4:
time: 167 us; the launch traced here: 166 us
  Pallas kernels  145 us (87%)
  other arithmetic  12.3 us (7%)
  matrix products  4.73 us (3%)
  local copies, waits for them, and re-layouts  3.79 us (2%)
    pallas_call x1, Pallas kernels, spread_rows(): pl.pallas_call(kernel, out_shape=jax.ShapeDtypeStruct((kinds, seq_count *...  49.2 us
    pallas_call x3, Pallas kernels, exchange(): pl.pallas_call(kernel, out_shape=jax.ShapeDtypeStruct(out_shape, x.dtype)...  46.5 us
    pallas_call x1, Pallas kernels, return_rows(): pl.pallas_call(kernel, out_shape=jax.ShapeDtypeStruct((capacity, width),...  44.6 us
    dot_general x2, matrix products, pick(): lax.dot_general(choice, rows, (((side,), (0,)), ((), ())), preferred_elem...  4.73 us
    pallas_call x1, Pallas kernels, attend(): pl.pallas_call(kernel, grid=(heads, rows // block), out_shape=jax.ShapeDt...  4.69 us
    sin x1, other arithmetic, position_table(): return jnp.concatenate([jnp.sin(angles), jnp.cos(angles)], axis=1)  3.69 us

profile of v4, /device:TPU:0, one launch (start us, length us, event | category | flops | bytes accessed | tf_op | source)
XLA Modules:
  0.0 165.9 jit_solution(3602680798179173606)
XLA Ops:
  0.0 0.0 copy-start
  0.0 1.4 reduce_sum.54
  1.4 1.1 broadcast_in_dim.113.x_ref
  2.5 0.7 broadcast_compare_fusion
  3.2 0.7 convert_element_type.26
  3.9 0.7 broadcast_compare_fusion.1
  4.5 0.8 select_reduce_fusion
  5.3 11.3 %shard_map.100 = s32[32,1,128]{2,1,0:T(1,128)} custom-call(s32[1,128]{1,0:T(1,128)} %broadcast_in_dim.113.x_ref), custom_call_target="tpu_custom_call" | custom-call | tf_op jit(solution)/shard_map/pallas_call | solution.py:90
  16.6 1.4 slice_reduce_fusion
  18.0 0.6 fusion.19
  18.7 1.3 add_select_fusion
  20.0 0.1 select_reduce_fusion.1
  20.1 0.1 broadcast_in_dim.121
  20.2 0.1 reshape.86
  20.3 0.1 broadcast_in_dim.120
  20.3 0.1 reshape.85
  20.5 0.6 fusion.17.choice_ref
  21.1 0.7 fusion.14.choice_ref
  21.8 0.9 fusion.26
  22.6 3.7 %multiply_sine_fusion = (f32[128,2048]{1,0:T(8,128)S(1)}, f32[128,2048]{1,0:T(8,128)S(1)}) fusion(f32[2048]{0:T(1024)S(1)} %multiply_exponential_fusion, f32[128]{0:T(128)S(1)} %convert_element_type.26), kind=kLoop, calls=%fused_computation.15 | loop fusion | flops 262144 | bytes 2105856 | tf_op jit(solution)/shard_map/sin | solution.py:21
  26.3 0.0 copy-done
  26.3 0.0 copy-start.2
  26.3 0.0 copy-start.3
  26.4 0.7 convert_reduce_fusion
  27.0 0.4 fusion.3
  27.5 0.0 copy-done.2
  27.5 0.0 copy-done.3
  27.5 1.7 %convolution_convert_fusion.x_ref = bf16[128,4096]{1,0:T(8,128)(2,1)} fusion(bf16[128,4096]{1,0:T(8,128)(2,1)S(1)} %get-tuple-element.6, f32[4096]{0:T(1024)S(1)} %copy-done.2, f32[4096]{0:T(1024)S(1)} %copy-done.3, f32[128]{0:T(128)S(1)} %add_rsqrt_fusion, f32[128]{0:T(128)S(1)} %broadcast_multiply_fusion, s32[128]{0:T(128)S(1)} %add_select_fusion), kind=kOutput, calls=%fused_computation.2 | convolution fusion | flops 137904128 | bytes 2131456 | tf_op jit(solution)/shard_map/dot_general | solution.py:599
  29.2 49.2 %shard_map.101.x_ref = bf16[3,256,512]{2,1,0:T(8,128)(2,1)} custom-call(bf16[128,4096]{1,0:T(8,128)(2,1)} %convolution_convert_fusion.x_ref, bf16[32,128]{1,0:T(8,128)(2,1)} %fusion.17.choice_ref, bf16[3,4096,512]{2,1,0:T(8,128)(2,1)} %w_hbm.1), custom_call_target="tpu_custom_call" | custom-call | tf_op jit(solution)/shard_map/pallas_call | solution.py:272
  78.4 21.3 %shard_map.102 = bf16[3,1024,128]{2,1,0:T(8,128)(2,1)} custom-call(bf16[3,256,512]{2,1,0:T(8,128)(2,1)} %shard_map.101.x_ref), custom_call_target="tpu_custom_call" | custom-call | tf_op jit(solution)/shard_map/pallas_call | solution.py:90
  99.7 4.7 %shard_map.103 = bf16[1,1024,128]{2,1,0:T(8,128)(2,1)} custom-call(bf16[3,1,1024,128]{3,2,1,0:T(8,128)(2,1)} %bitcast.5, bf16[3,1,1024,128]{3,2,1,0:T(8,128)(2,1)} %bitcast.6, bf16[3,1,1024,128]{3,2,1,0:T(8,128)(2,1)} %bitcast.7), custom_call_target="tpu_custom_call" | custom-call | tf_op jit(solution)/shard_map/pallas_call | solution.py:472
  104.3 13.9 %shard_map.104.x_ref = bf16[256,512]{1,0:T(8,128)(2,1)} custom-call(bf16[1024,128]{1,0:T(8,128)(2,1)} %bitcast.8), custom_call_target="tpu_custom_call" | custom-call | tf_op jit(solution)/shard_map/pallas_call | solution.py:90
  118.2 0.0 copy-start.1
  118.2 44.6 %shard_map.105 = bf16[128,4096]{1,0:T(8,128)(2,1)} custom-call(bf16[256,512]{1,0:T(8,128)(2,1)} %shard_map.104.x_ref, bf16[512,4096]{1,0:T(8,128)(2,1)} %w_ref.1, bf16[128,32]{1,0:T(8,128)(2,1)} %fusion.14.choice_ref), custom_call_target="tpu_custom_call" | custom-call | tf_op jit(solution)/shard_map/pallas_call | solution.py:429
  162.9 0.0 copy-done.1
  162.9 3.0 %fusion = f32[128,4096]{1,0:T(8,128)} fusion(bf16[128,4096]{1,0:T(8,128)(2,1)} %shard_map.105, bf16[128,4096]{1,0:T(8,128)(2,1)S(1)} %get-tuple-element.6, f32[4096]{0:T(1024)S(1)} %copy-done.1, pred[128]{0:T(512)(128)(4,1)S(1)} %broadcast_compare_fusion.1, s32[128]{0:T(128)S(1)} %add_select_fusion), kind=kOutput, calls=%fused_computation.1 | convolution fusion | flops 135806976 | bytes 4211328 | tf_op jit(solution)/shard_map/dot_general | solution.py:599
  (4 shorter events, 0.0 us)
Async XLA Ops:
  0.0 26.3 %copy-start = (bf16[128,4096]{1,0:T(8,128)(2,1)S(1)}, bf16[128,4096]{1,0:T(8,128)(2,1)}, u32[]{:S(2)}) copy-start(bf16[128,4096]{1,0:T(8,128)(2,1)} %param.10) | copy-start | bytes 3145732
  26.3 1.1 copy-start.2
  26.3 1.1 copy-start.3
  118.2 44.7 %copy-start.1 = (f32[4096]{0:T(1024)S(1)}, f32[4096]{0:T(1024)}, u32[]{:S(2)}) copy-start(f32[4096]{0:T(1024)} %param.19) | copy-start | bytes 49156
